TPU v7x, 32 devices: a whole 2x2x4 slice. The times are simulated.
32 devices in a mesh: grp: 4 (over z), dev: 8 (over y, x, core).
Axes of the slice: x: 2, y: 2, z: 4, core: 2. Of those that a mesh axis runs over, the one named last changes fastest.
Arguments:
- feats: bfloat16 [8192, 1024], P(('grp', 'dev')), may hold values from -6 to 6
- weight: float32 [1024, 1024], replicated, may hold values from -0.1875 to 0.1875
- cotangent: bfloat16 [8192, 1024], P(('grp', 'dev')), may hold values from -6 to 6
- local_adj: int32 [8192, 256], P(('grp', 'dev')), may hold values 0 or 1
- far_mask: int32 [4, 8, 4, 8, 256], P('grp', 'dev'), may hold values 0 or 1
- far_row: int32 [4, 8, 4, 8], P('grp', 'dev'), may hold values from 0 to 255
Outputs:
- activated: bfloat16 [8192, 1024], P(('grp', 'dev'))
- input_grad: float32 [8192, 1024], P(('grp', 'dev'))
- weight_grad: float32 [1024, 1024], P('dev')
All inputs are finite; a program needn't handle non-finite values. No bound on the sum of `local_adj` or of `far_mask` on one device may be relied on, other than what follows from the above.
Results may differ from a plain program's by a relative error of at most 0.001.
Values sent between devices are 32-bit elements; how exact they have to be, the bound alone decides.
No kernel may reach another device: no remote copies, remote signals or barrier semaphores. Data moves between devices by JAX's collectives and lax.ppermute only.
A program may use at most 64 MiB of HBM per device.

v0:
```python
import jax
import jax.numpy as jnp
from jax import lax
from jax.sharding import PartitionSpec as P


def contract_first(left_side, right_side):
    return lax.dot_general(
        left_side,
        right_side,
        (((0,), (0,)), ((), ())),
        precision=lax.Precision.HIGHEST,
        preferred_element_type=jnp.float32,
    )


def contract_last(left_side, right_side):
    return lax.dot_general(
        left_side,
        right_side,
        (((1,), (1,)), ((), ())),
        precision=lax.Precision.HIGHEST,
        preferred_element_type=jnp.float32,
    )


def body(feats, weight, cotangent, local_adj, far_mask, far_row):
    highest = lax.Precision.HIGHEST
    node_count = feats.shape[0]
    groups = lax.axis_size("grp")
    slot_width = far_mask.shape[3]
    slot_total = groups * slot_width
    border_mask = far_mask.reshape(slot_total, node_count).astype(jnp.float32)
    slot_counts = jnp.sum(border_mask, axis=1).reshape(groups, slot_width)
    adjacency = local_adj.astype(jnp.float32)
    node_index = lax.broadcasted_iota(jnp.int32, (node_count, slot_total), 0)
    one_hot = (far_row.reshape(1, slot_total) == node_index).astype(jnp.float32)
    feats_wide = feats.astype(jnp.float32)
    outgoing = jnp.dot(border_mask.astype(jnp.bfloat16), feats, preferred_element_type=jnp.float32)
    local_sum = jnp.dot(local_adj.astype(jnp.bfloat16), feats, preferred_element_type=jnp.float32)
    received, arrived_counts = (
        lax.all_to_all(
            outgoing.reshape(groups, slot_width, outgoing.shape[1]),
            "grp",
            split_axis=0,
            concat_axis=0,
            tiled=True,
        ),
        lax.all_to_all(slot_counts, "grp", split_axis=0, concat_axis=0, tiled=True),
    )
    remote_sum = jnp.dot(
        one_hot,
        received.reshape(slot_total, received.shape[2]),
        precision=highest,
        preferred_element_type=jnp.float32,
    )
    degree = jnp.sum(adjacency, axis=1) + jnp.dot(
        one_hot,
        arrived_counts.reshape(slot_total),
        precision=highest,
        preferred_element_type=jnp.float32,
    )
    inverse = 1.0 / (1.0 + degree)
    combined = (feats_wide + local_sum + remote_sum) * inverse[:, None]
    preact = jnp.dot(combined, weight, precision=highest, preferred_element_type=jnp.float32)
    sigmoid_pre = jax.nn.sigmoid(preact)
    activated = (preact * sigmoid_pre).astype(jnp.bfloat16)
    pre_grad = cotangent.astype(jnp.float32) * sigmoid_pre * (1.0 + preact * (1.0 - sigmoid_pre))
    scaled_grad = contract_last(pre_grad, weight) * inverse[:, None]
    slot_rows = contract_first(one_hot, scaled_grad).reshape(
        groups, slot_width, scaled_grad.shape[1]
    )
    returned = lax.all_to_all(slot_rows, "grp", split_axis=0, concat_axis=0, tiled=True)
    back_total = scaled_grad + contract_first(adjacency, scaled_grad)
    back_total = back_total + contract_first(
        border_mask, returned.reshape(slot_total, returned.shape[2])
    )
    weight_shard = lax.psum_scatter(
        contract_first(combined, pre_grad), "dev", scatter_dimension=0, tiled=True
    )
    weight_grad = lax.psum(weight_shard, "grp")
    return (activated, back_total, weight_grad)


def solution(mesh):
    in_specs = (
        P(("grp", "dev"), None),
        P(),
        P(("grp", "dev"), None),
        P(("grp", "dev"), None),
        P("grp", "dev", None, None, None),
        P("grp", "dev", None, None),
    )
    out_specs = (P(("grp", "dev"), None), P(("grp", "dev"), None), P("dev", None))
    return jax.shard_map(body, mesh=mesh, in_specs=in_specs, out_specs=out_specs, check_vma=False)
```

profile of v0, /device:TPU:0, one launch (start us, length us, event | category | flops | bytes accessed | tf_op | source)
XLA Modules:
  0.0 144.3 jit_solution(8972619024536431822)
XLA Ops:
  7.2 1.4 convert_reduce_fusion.1
  8.6 6.3 %all-to-all-start.1 = ((f32[4,1,8]{2,1,0:T(1,128)}), f32[4,1,8]{2,1,0:T(1,128)S(1)}, u32[]{:S(2)}, u32[]{:S(2)}) async-start(f32[4,1,8]{2,1,0:T(1,128)} %bitcast.4), calls=%async_computation.1 | async-start | bytes 4096 | tf_op jit(solution)/shard_map/all_to_all | solution.py:49
  14.9 1.9 %fusion.3 = f32[4,8,1024]{2,1,0:T(8,128)} fusion(bf16[256,1024]{1,0:T(8,128)(2,1)} %param.6, s32[1,1,4,8,256]{4,3,2,1,0:T(8,128)} %param.10), kind=kOutput, calls=%fused_computation.12 | convolution fusion | flops 16793600 | bytes 688128 | tf_op jit(solution)/shard_map/dot_general | solution.py:39
  16.8 1.6 %convolution_add_fusion.1 = f32[256,1024]{1,0:T(8,128)S(1)} fusion(bf16[256,1024]{1,0:T(8,128)(2,1)} %param.6, s32[256,256]{1,0:T(8,128)} %param.9), kind=kOutput, calls=%fused_computation.7 | convolution fusion | flops 134807552 | bytes 1835008 | tf_op jit(solution)/shard_map/dot_general | solution.py:40
  18.5 1.1 convert_reduce_fusion
  19.5 0.8 eq.10
  20.3 0.1 all-to-all-done.1
  20.4 5.0 %all-to-all-start = ((f32[4,8,1024]{2,1,0:T(8,128)}), f32[4,8,1024]{2,1,0:T(8,128)S(1)}, u32[]{:S(2)}, u32[]{:S(2)}) async-start(f32[4,8,1024]{2,1,0:T(8,128)} %fusion.3), calls=%async_computation | async-start | bytes 262144 | tf_op jit(solution)/shard_map/all_to_all | solution.py:42
  25.4 0.0 reduce-scatter.2.cloned.1.call-start
  25.4 0.5 broadcast.17
  25.9 0.7 reduce.4
  26.6 0.1 reshape.40
  26.7 0.1 fusion.8
  26.8 0.0 copy-start.1
  26.9 4.5 %all-to-all-done = f32[4,8,1024]{2,1,0:T(8,128)S(1)} async-done(((f32[4,8,1024]{2,1,0:T(8,128)}), f32[4,8,1024]{2,1,0:T(8,128)S(1)}, u32[]{:S(2)}, u32[]{:S(2)}) %all-to-all-start) | async-done | bytes 131104 | tf_op jit(solution)/shard_map/all_to_all | solution.py:42
  31.3 0.6 fusion.2
  31.9 6.7 %multiply_convert_fusion = (bf16[256,1024]{1,0:T(8,128)(2,1)}, f32[256,1024]{1,0:T(8,128)S(1)}) fusion(f32[256,1024]{1,0:T(8,128)S(1)} %fusion.2, f32[1024,1024]{1,0:T(8,128)} %param.7), kind=kOutput, calls=%fused_computation.10 | convolution fusion | flops 3222536192 | bytes 6815744 | tf_op jit(solution)/shard_map/dot_general | solution.py:65
  38.7 0.0 copy-done.1
  38.7 5.5 %fusion.17 = f32[1024,1024]{1,0:T(8,128)} fusion(f32[256,1024]{1,0:T(8,128)S(1)} %fusion.2, f32[256,1024]{1,0:T(8,128)S(1)} %get-tuple-element.4, bf16[256,1024]{1,0:T(8,128)(2,1)S(1)} %copy-done.1), kind=kOutput, calls=%fused_computation.30 | convolution fusion | flops 3223584768 | bytes 6815744 | tf_op jit(solution)/shard_map/dot_general | solution.py:8
  44.2 0.0 reduce-scatter.2.cloned.1.call-update
  44.2 0.0 copy-start
  44.2 0.0 copy-start.2
  44.2 6.6 %convolution_multiply_fusion = f32[256,1024]{1,0:T(8,128)S(1)} fusion(f32[1024,1024]{1,0:T(8,128)} %param.7, f32[256]{0:T(256)S(1)} %add_divide_fusion.1, f32[256,1024]{1,0:T(8,128)S(1)} %get-tuple-element.4, bf16[256,1024]{1,0:T(8,128)(2,1)S(1)} %copy-done.1), kind=kOutput, calls=%fused_computation.4 | convolution fusion | flops 3223846912 | bytes 6816768 | tf_op jit(solution)/shard_map/dot_general | solution.py:18
  50.8 1.2 convolution_bitcast_fusion.2
  52.0 3.3 %all-to-all-start.2 = ((f32[4,8,1024]{2,1,0:T(8,128)}), f32[4,8,1024]{2,1,0:T(8,128)S(1)}, u32[]{:S(2)}, u32[]{:S(2)}) async-start(f32[4,8,1024]{2,1,0:T(8,128)} %convolution_bitcast_fusion.2), calls=%async_computation.2 | async-start | bytes 262144 | tf_op jit(solution)/shard_map/all_to_all | solution.py:73
  55.3 0.0 all-reduce.2.cloned.1.call-start
  55.4 39.2 %reduce-scatter.2.cloned.1.call-done = f32[128,1024]{1,0:T(8,128)} async-done(((f32[1024,1024]{1,0:T(8,128)}), f32[128,1024]{1,0:T(8,128)}) %reduce-scatter.2.cloned.1.call-update) | async-done | bytes 524304 | tf_op jit(solution)/shard_map/reduce_scatter | solution.py:78
  94.6 0.0 all-reduce.2.cloned.1.call-update
  94.6 0.0 copy-done
  94.6 1.1 fusion.1
  95.7 0.0 all-to-all-done.2
  95.7 0.0 copy-done.2
  95.7 2.0 %fusion = f32[256,1024]{1,0:T(8,128)} fusion(f32[256,1024]{1,0:T(8,128)S(1)} %fusion.1, f32[4,8,1024]{2,1,0:T(8,128)S(1)} %all-to-all-done.2, s32[1,1,4,8,256]{4,3,2,1,0:T(8,128)S(1)} %copy-done.2), kind=kOutput, calls=%fused_computation.1 | convolution fusion | flops 100933632 | bytes 2260992 | tf_op jit(solution)/shard_map/dot_general | solution.py:8
  97.7 37.9 %all-reduce.2.cloned.1.call-done = f32[128,1024]{1,0:T(8,128)} async-done(((f32[128,1024]{1,0:T(8,128)}), f32[128,1024]{1,0:T(8,128)}) %all-reduce.2.cloned.1.call-update) | async-done | bytes 524304 | tf_op jit(solution)/shard_map/psum | solution.py:81
  135.6 1.9 %copy.17 = f32[128,1024]{1,0:T(8,128)} copy(f32[128,1024]{1,0:T(8,128)} %all-reduce.2.cloned.1.call-done) | data formatting | bytes 1048576
  (1 shorter events, 0.0 us)
Async XLA Ops:
  8.6 11.8 %all-to-all-start.1 = ((f32[4,1,8]{2,1,0:T(1,128)}), f32[4,1,8]{2,1,0:T(1,128)S(1)}, u32[]{:S(2)}, u32[]{:S(2)}) async-start(f32[4,1,8]{2,1,0:T(1,128)} %bitcast.4), calls=%async_computation.1 | async-start | bytes 4096 | tf_op jit(solution)/shard_map/all_to_all | solution.py:49
  20.4 10.9 %all-to-all-start = ((f32[4,8,1024]{2,1,0:T(8,128)}), f32[4,8,1024]{2,1,0:T(8,128)S(1)}, u32[]{:S(2)}, u32[]{:S(2)}) async-start(f32[4,8,1024]{2,1,0:T(8,128)} %fusion.3), calls=%async_computation | async-start | bytes 262144 | tf_op jit(solution)/shard_map/all_to_all | solution.py:42
  25.4 69.2 %reduce-scatter.2.cloned.1.call-start = ((), (), s32[]{:S(2)}) async-start(), calls=%async_computation.4 | async-start | bytes 4718592 | tf_op jit(solution)/shard_map/reduce_scatter | solution.py:78
  26.8 11.9 %copy-start.1 = (bf16[256,1024]{1,0:T(8,128)(2,1)S(1)}, bf16[256,1024]{1,0:T(8,128)(2,1)}, u32[]{:S(2)}) copy-start(bf16[256,1024]{1,0:T(8,128)(2,1)} %param.8) | copy-start | bytes 1572868
  44.2 50.4 %copy-start = (s32[256,256]{1,0:T(8,128)S(1)}, s32[256,256]{1,0:T(8,128)}, u32[]{:S(2)}) copy-start(s32[256,256]{1,0:T(8,128)} %param.9) | copy-start | bytes 786436
  44.2 51.5 %copy-start.2 = (s32[1,1,4,8,256]{4,3,2,1,0:T(8,128)S(1)}, s32[1,1,4,8,256]{4,3,2,1,0:T(8,128)}, u32[]{:S(2)}) copy-start(s32[1,1,4,8,256]{4,3,2,1,0:T(8,128)} %param.10) | copy-start | bytes 98308
  52.0 43.7 %all-to-all-start.2 = ((f32[4,8,1024]{2,1,0:T(8,128)}), f32[4,8,1024]{2,1,0:T(8,128)S(1)}, u32[]{:S(2)}, u32[]{:S(2)}) async-start(f32[4,8,1024]{2,1,0:T(8,128)} %convolution_bitcast_fusion.2), calls=%async_computation.2 | async-start | bytes 262144 | tf_op jit(solution)/shard_map/all_to_all | solution.py:73
  55.3 80.3 %all-reduce.2.cloned.1.call-start = ((), (), s32[]{:S(2)}) async-start(), calls=%async_computation.5 | async-start | bytes 1048576 | tf_op jit(solution)/shard_map/psum | solution.py:81
Sparse Core Ops, SparseCore 0:
  44.3 50.2 reduce-scatter.1
  96.9 38.6 all-reduce.1
where the time goes:
time: 145 us; the launch traced here: 144 us
  waiting for transfers between devices  81.7 us (56%)
  matrix products  27.3 us (19%)
  starting transfers between devices  14.7 us (10%)
  between operations  14.2 us (10%)
  local copies, waits for them, and re-layouts  3.29 us (2%)
  other arithmetic  3.16 us (2%)
    reduce_scatter x1, waiting for transfers between devices, body(): lax.psum_scatter(contract_first(combined, pre_grad), 'dev', scatter_dimen...  39.2 us
    psum x1, waiting for transfers between devices, body(): weight_grad = lax.psum(weight_shard, 'grp')  37.9 us
    dot_general x4, matrix products, contract_first(): lax.dot_general(left_side, right_side, (((0,), (0,)), ((), ())), precisio...  9.77 us
    dot_general x1, matrix products, body(): jnp.dot(combined, weight, precision=highest, preferred_element_type=jnp.f...  6.75 us
    dot_general x1, matrix products, contract_last(): lax.dot_general(left_side, right_side, (((1,), (1,)), ((), ())), precisio...  6.58 us
    all_to_all x1, starting transfers between devices, body(): lax.all_to_all(slot_counts, 'grp', split_axis=0, concat_axis=0, tiled=True)  6.35 us
    all_to_all x1, starting transfers between devices, body(): lax.all_to_all(outgoing.reshape(groups, slot_width, outgoing.shape[1]), '...  4.96 us
    all_to_all x1, waiting for transfers between devices, body(): lax.all_to_all(outgoing.reshape(groups, slot_width, outgoing.shape[1]), '...  4.45 us
  transfers between devices with their start and end apart: 5, of which 4 were waited for; matrix products, arithmetic and copies ran while one was open for 12% of the time, Pallas kernels for 0%

commit v1 on v0

v1 whole, which is shorter than its diff:
```python
import functools

import jax
import jax.numpy as jnp
from jax import lax
from jax.experimental import pallas as pl
from jax.experimental.pallas import tpu as pltpu
from jax.sharding import PartitionSpec as P


AXES = ("grp", "dev")
LANES = 128
EIGHTHS = (4, 4)
CHUNKS = len(EIGHTHS)
LIMIT = 16 << 20
F32 = jnp.float32
BF16 = jnp.bfloat16
VMEM = pl.BlockSpec(memory_space=pltpu.VMEM)
SMEM = pl.BlockSpec(memory_space=pltpu.SMEM)
HBM = pl.BlockSpec(memory_space=pltpu.HBM)


def in_hbm(value):
    return pltpu.with_memory_space_constraint(value, pltpu.HBM)


def split(value):
    high = value.astype(BF16)
    return high, (value - high.astype(F32)).astype(BF16)


def dot(left, right, dims=((1,), (0,))):
    return lax.dot_general(left, right, (dims, ((), ())), preferred_element_type=F32)


def dot_three(left, right, dims=((1,), (0,))):
    left_high, left_low = left
    right_high, right_low = right
    return dot(left_high, right_high, dims) + (
        dot(left_high, right_low, dims) + dot(left_low, right_high, dims)
    )


def call(kernel, out_shape, in_specs, flops, bytes_moved, scratch=(), outs=None, aliases=None):
    many = isinstance(out_shape, (tuple, list))
    return pl.pallas_call(
        kernel,
        out_shape=out_shape,
        in_specs=in_specs,
        out_specs=outs or ([VMEM] * len(out_shape) if many else VMEM),
        input_output_aliases=aliases or {},
        scratch_shapes=list(scratch),
        compiler_params=pltpu.CompilerParams(vmem_limit_bytes=LIMIT),
        cost_estimate=pl.CostEstimate(
            flops=flops, bytes_accessed=bytes_moved, transcendentals=0
        ),
    )


def border_kernel(groups, width, me_ref, feats_hbm, mask_hbm, *refs):
    out_refs, (feats_ref, mask_ref, sems) = refs[:groups], refs[groups:]
    copies = [
        pltpu.make_async_copy(source, target, sems.at[k])
        for k, (source, target) in enumerate(
            ((feats_hbm, feats_ref), (mask_hbm, mask_ref))
        )
    ]
    for copy in copies:
        copy.start()
    for copy in copies:
        copy.wait()
    feats = feats_ref[...]
    lanes = feats.shape[1]
    for step, out_ref in enumerate(out_refs):
        target = lax.rem(me_ref[0] + step, groups)
        flags = mask_ref[pl.ds(pl.multiple_of(target * width, width), width), :]
        flags = flags.astype(F32)
        out_ref[:, :lanes] = dot(flags.astype(BF16), feats)
        counts = jnp.sum(flags, axis=1, keepdims=True)
        out_ref[:, lanes:] = jnp.broadcast_to(counts, (width, LANES))


def local_kernel(
    pieces, feats_hbm, adj_hbm, weight_hbm, base_ref, degree_ref, high_ref, low_ref,
    feats_ref, adj_ref, weight_ref, sems,
):
    step = weight_hbm.shape[0] // pieces
    copies = [
        pltpu.make_async_copy(feats_hbm, feats_ref, sems.at[0]),
        pltpu.make_async_copy(adj_hbm, adj_ref, sems.at[1]),
    ]
    for k in range(pieces):
        rows = pl.ds(k * step, step)
        copies.append(
            pltpu.make_async_copy(
                weight_hbm.at[rows, :], weight_ref.at[rows, :], sems.at[2 + k]
            )
        )
    for copy in copies:
        copy.start()
    copies[0].wait()
    copies[1].wait()
    feats = feats_ref[...]
    flags = adj_ref[...].astype(F32)
    base_ref[...] = feats.astype(F32) + dot(flags.astype(BF16), feats)
    degree = jnp.sum(flags, axis=1, keepdims=True)
    degree_ref[...] = jnp.broadcast_to(degree, degree_ref.shape)
    for k in range(pieces):
        copies[2 + k].wait()
        rows = pl.ds(k * step, step)
        high, low = split(weight_ref[rows, :])
        high_ref[rows, :] = high
        low_ref[rows, :] = low


def aggregate_kernel(groups, parts, orders, grp_ref, dev_ref, rows_ref, base_ref, degree_ref, *refs):
    arrived = jnp.concatenate([ref[...] for ref in refs[:groups]], axis=0)
    agg_ref, inverse_ref, hot_ref = refs[groups : groups + 3]
    flipped, turned_ref, flags_ref = refs[groups + 3 : -2], refs[-2], refs[-1]
    nodes, lanes = base_ref.shape
    width = rows_ref.shape[1]
    index = lax.broadcasted_iota(jnp.int32, (1, nodes), 1)
    for step in range(groups):
        source = lax.rem(grp_ref[0] + (groups - step), groups)
        for slot in range(width):
            at = step * width + slot
            flags_ref[at : at + 1, :] = jnp.where(index == rows_ref[source, slot], 1.0, 0.0)
    one_hot = flags_ref[...].astype(BF16)
    hot_ref[...] = one_hot
    high, low = split(arrived)
    first = ((0,), (0,))
    remote = dot(one_hot, high, first) + dot(one_hot, low, first)
    inverse = 1.0 / (1.0 + degree_ref[...] + remote[:, lanes:])
    inverse_ref[...] = inverse
    agg = (base_ref[...] + remote[:, :lanes]) * inverse[:, :1]
    agg_ref[...] = agg
    turned_ref[...] = agg.T
    for which, ref in enumerate(flipped):
        for place, block in enumerate(orders(dev_ref[0], which)):
            picked = turned_ref[pl.ds(pl.multiple_of(block * parts, parts), parts), :]
            ref[place * parts : (place + 1) * parts, :] = picked


def forward_kernel(start, agg_ref, high_ref, low_ref, cot_ref, act_ref, grad_ref):
    at = slice(start, start + act_ref.shape[1])
    preact = dot_three(split(agg_ref[...]), (high_ref[:, at], low_ref[:, at]))
    sigmoid = 1.0 / (1.0 + jnp.exp(-preact))
    act_ref[...] = (preact * sigmoid).astype(BF16)
    slope = sigmoid * (1.0 + preact * (1.0 - sigmoid))
    grad_ref[...] = cot_ref[:, at].astype(F32) * slope


def term_kernel(count, *refs):
    total = None
    for agg_ref, grad_ref in zip(refs[:count], refs[count : 2 * count]):
        part = dot_three(split(agg_ref[...]), split(grad_ref[...]))
        total = part if total is None else total + part
    outs = refs[2 * count :]
    start = 0
    for ref in outs:
        ref[...] = total[start : start + ref.shape[0]]
        start += ref.shape[0]


def slots_kernel(width, hot_ref, inverse_ref, *refs):
    grads, acts = refs[:CHUNKS], refs[CHUNKS : 2 * CHUNKS]
    outs, act_ref = refs[2 * CHUNKS : -1], refs[-1]
    one_hot = hot_ref[...]
    start = 0
    for ref, act in zip(grads, acts):
        stop = start + ref.shape[1]
        act_ref[:, start:stop] = act[...]
        high, low = split(ref[...] * inverse_ref[:, :1])
        rows = dot(one_hot, high) + dot(one_hot, low)
        for step, out in enumerate(outs):
            out[:, start:stop] = rows[step * width : (step + 1) * width]
        start = stop


def last_kernel(start, count, total_ref, *refs):
    came, (out_ref, sum_ref, sem) = refs[:count], refs[-3:]
    total = total_ref[...]
    for ref in came:
        total = total + ref[...]
    sum_ref[...] = total
    columns = pl.ds(start, total.shape[1])
    copy = pltpu.make_async_copy(sum_ref, out_ref.at[:, columns], sem)
    copy.start()
    copy.wait()


def backward_kernel(
    groups, width, me_ref, adj_ref, mask_ref, inverse_ref, high_ref, low_ref, *refs
):
    grads, refs = refs[:CHUNKS], refs[CHUNKS:]
    arrived, out_ref = refs[:groups], refs[groups]
    flags = adj_ref[...].astype(F32).T.astype(BF16)
    pieces = [
        mask_ref[pl.ds(pl.multiple_of(lax.rem(me_ref[0] + s, groups) * width, width), width), :]
        for s in range(groups)
    ]
    border = jnp.concatenate(pieces, axis=0).astype(F32).T.astype(BF16)
    total, start = None, 0
    for ref in grads:
        stop = start + ref.shape[1]
        scaled = ref[...] * inverse_ref[:, :1]
        high, low = split(scaled)
        back = scaled + dot(flags, high) + dot(flags, low)
        high, low = split(jnp.concatenate([r[:, start:stop] for r in arrived], axis=0))
        back = back + dot(border, high) + dot(border, low)
        part = dot_three(split(back), (high_ref[:, start:stop], low_ref[:, start:stop]), ((1,), (1,)))
        total = part if total is None else total + part
        start = stop
    out_ref[...] = total


def factors(number):
    found, prime = [], 2
    while number > 1:
        while number % prime == 0:
            found.append(prime)
            number //= prime
        prime += 1
    return found


def stages_of(number):
    stages, stride = [], 1
    for factor in factors(number):
        stages.append((stride, factor))
        stride *= factor
    return stages


def turned(stages, shift):
    run = 0
    while run < len(stages) and stages[run][1] == stages[0][1]:
        run += 1
    shift = shift % run if run else 0
    return stages[shift:run] + stages[:shift] + stages[run:]


def shifted(index, stage, amount):
    stride, factor = stage
    if isinstance(index, int):
        digit = index // stride % factor
        return index + ((digit + amount) % factor - digit) * stride
    digit = lax.rem(lax.div(index, stride), factor)
    return index + (lax.rem(digit + amount, factor) - digit) * stride


def pick(condition_index, values):
    result = values[0]
    for place, value in enumerate(values[1:], 1):
        result = jnp.where(condition_index == place, value, result)
    return result


def body(groups, devs, feats, weight, cotangent, local_adj, far_mask, far_row):
    nodes, lanes = feats.shape
    width = far_mask.shape[3]
    slots = groups * width
    outer = weight.shape[1]
    share = weight.shape[0] // devs
    edges = [outer * sum(EIGHTHS[:c]) // sum(EIGHTHS) for c in range(CHUNKS + 1)]
    me_grp, me_dev = lax.axis_index("grp"), lax.axis_index("dev")
    me = me_grp.reshape(1).astype(jnp.int32)
    dev = me_dev.reshape(1).astype(jnp.int32)
    mask = far_mask.reshape(slots, nodes)
    shape = jax.ShapeDtypeStruct

    def permute(value, pairs):
        return lax.ppermute(value, AXES, pairs)

    def over_grp(step):
        return [
            (g * devs + d, ((g + step) % groups) * devs + d)
            for g in range(groups)
            for d in range(devs)
        ]

    def over(moves):
        return [
            (g * devs + d, moves(g, d)[0] * devs + moves(g, d)[1])
            for g in range(groups)
            for d in range(devs)
        ]

    stages = stages_of(devs)
    first, rest = stages[0], stages[1:]
    pair = first[1]
    kinds = [turned(rest, k) for k in range(pair)]
    grp_kinds = [turned(stages_of(groups), k) for k in range(pair)]
    inner = devs // pair

    def orders(dev, which):
        dev = shifted(dev, first, which)
        lists = []
        for kind in kinds:
            found = [dev]
            for stage in reversed(kind):
                found = [shifted(d, stage, e) for e in range(stage[1]) for d in found]
            lists.append(found)
        return [pick(lax.rem(dev, pair), same) for same in zip(*lists)]

    outgoing = call(
        functools.partial(border_kernel, groups, width),
        [shape((width, lanes + LANES), F32)] * groups,
        [SMEM, HBM, HBM],
        2 * slots * nodes * lanes,
        feats.size * 2 + mask.size * 4,
        [
            pltpu.VMEM(feats.shape, BF16),
            pltpu.VMEM(mask.shape, jnp.int32),
            pltpu.SemaphoreType.DMA((2,)),
        ],
    )(me, in_hbm(feats), in_hbm(mask))
    received = [outgoing[0]] + [
        permute(outgoing[k], over_grp(k)) for k in range(1, groups)
    ]
    pieces = 4
    base, degree, high, low = call(
        functools.partial(local_kernel, pieces),
        [shape((nodes, lanes), F32), shape((nodes, LANES), F32)]
        + [shape(weight.shape, BF16)] * 2,
        [HBM, HBM, HBM],
        2 * nodes * nodes * lanes,
        nodes * lanes * 6 + weight.size * 8,
        [
            pltpu.VMEM(feats.shape, BF16),
            pltpu.VMEM(local_adj.shape, jnp.int32),
            pltpu.VMEM(weight.shape, F32),
            pltpu.SemaphoreType.DMA((2 + pieces,)),
        ],
    )(in_hbm(feats), in_hbm(local_adj), in_hbm(weight))
    agg, inverse, hot, *flipped = call(
        functools.partial(aggregate_kernel, groups, share, orders),
        [
            shape((nodes, lanes), F32),
            shape((nodes, LANES), F32),
            shape((slots, nodes), BF16),
        ]
        + [shape((inner * share, nodes), F32)] * pair,
        [SMEM, SMEM, SMEM] + [VMEM] * (2 + groups),
        4 * slots * nodes * lanes,
        nodes * lanes * 16,
        [pltpu.VMEM((lanes, nodes), F32), pltpu.VMEM((slots, nodes), F32)],
    )(me, dev, far_row.reshape(groups, width), base, degree, *received)

    def to_partner(value, k):
        return permute(value, over(lambda g, d: (g, shifted(d, first, k))))

    aggs = [flipped[0]] + [to_partner(flipped[k], k) for k in range(1, pair)]

    acts, grads = [], []
    sends, keeps = [], []
    half = rest[0][1] if rest else 1
    block = inner * share // half
    for c in range(CHUNKS):
        piece = edges[c + 1] - edges[c]
        act, grad = call(
            functools.partial(forward_kernel, edges[c]),
            [shape((nodes, piece), BF16), shape((nodes, piece), F32)],
            [VMEM] * 4,
            6 * nodes * lanes * piece,
            lanes * piece * 4 + nodes * lanes * 4,
        )(agg, high, low, cotangent)
        acts.append(act)
        grads.append(grad)
    for c in range(CHUNKS):
        piece = edges[c + 1] - edges[c]
        chunk = [grads[c]] + [to_partner(grads[c], k) for k in range(1, pair)]
        outs = call(
            functools.partial(term_kernel, pair),
            [shape((block, piece), F32)] * half,
            [VMEM] * (2 * pair),
            6 * nodes * pair * inner * share * piece,
            inner * share * piece * 4 + nodes * pair * (piece + inner * share) * 4,
        )(*aggs, *chunk)
        keeps.append(outs[0])
        sends.append(outs[1:])

    totals = []
    for c in range(CHUNKS):
        keep, send = keeps[c], sends[c]
        for level in range(len(rest)):
            size = [kind[level][1] for kind in kinds][0]
            came = [
                permute(
                    send[k - 1], over(lambda g, d, k=k: (g, shifted(d, kinds[d % pair][level], k)))
                )
                for k in range(1, size)
            ]
            if level + 1 < len(rest):
                split_in = kinds[0][level + 1][1]
                step = keep.shape[0] // split_in
                parts = []
                for k in range(split_in):
                    at = slice(k * step, (k + 1) * step)
                    parts.append(functools.reduce(jnp.add, [keep[at]] + [v[at] for v in came]))
                keep, send = parts[0], parts[1:]
            else:
                keep = functools.reduce(jnp.add, [keep] + came)
        totals.append(keep)
    pick_slots = call(
        functools.partial(slots_kernel, width),
        [shape((width, outer), F32)] * groups + [shape((nodes, outer), BF16)],
        [VMEM] * (2 + 2 * CHUNKS),
        4 * slots * nodes * outer,
        nodes * outer * 4,
    )
    *slot_rows, activated = pick_slots(hot, inverse, *grads, *acts)
    weight_grad = None
    levels = len(grp_kinds[0])
    for level in range(levels):
        size = grp_kinds[0][level][1]
        for c in range(CHUNKS):
            came = [
                permute(
                    totals[c],
                    over(lambda g, d, k=k: (shifted(g, grp_kinds[d % pair][level], k), d)),
                )
                for k in range(1, size)
            ]
            if level + 1 < levels:
                totals[c] = functools.reduce(jnp.add, [totals[c]] + came)
                continue
            piece = edges[c + 1] - edges[c]
            before = [] if weight_grad is None else [weight_grad]
            weight_grad = call(
                functools.partial(last_kernel, edges[c], len(came)),
                shape((share, outer), F32),
                [VMEM] * (1 + len(came)) + [HBM] * len(before),
                share * piece,
                share * piece * 4,
                [pltpu.VMEM((share, piece), F32), pltpu.SemaphoreType.DMA],
                HBM,
                {1 + len(came): 0} if before else None,
            )(totals[c], *came, *before)
    returned = [slot_rows[0]] + [
        permute(slot_rows[k], over_grp(groups - k)) for k in range(1, groups)
    ]
    back = call(
        functools.partial(backward_kernel, groups, width),
        shape((nodes, lanes), F32),
        [SMEM] + [VMEM] * (5 + CHUNKS + groups),
        6 * nodes * lanes * outer,
        nodes * outer * 8 + weight.size * 4,
    )
    input_grad = back(me, local_adj, mask, inverse, high, low, *grads, *returned)
    return activated, input_grad, weight_grad


def solution(mesh):
    in_specs = (
        P(AXES, None),
        P(),
        P(AXES, None),
        P(AXES, None),
        P("grp", "dev", None, None, None),
        P("grp", "dev", None, None),
    )
    out_specs = (P(AXES, None), P(AXES, None), P("dev", None))
    groups, devs = mesh.shape["grp"], mesh.shape["dev"]

    def run(*args):
        return body(groups, devs, *args)

    return jax.shard_map(
        run, mesh=mesh, in_specs=in_specs, out_specs=out_specs, check_vma=False
    )
```

time: 145 us -> 75 us (0.52)
  waiting for transfers between devices: 81.7 us -> 34.9 us
  matrix products: 27.3 us -> 0 us
  Pallas kernels: 0 us -> 16.3 us
  between operations: 14.2 us -> 0.79 us
  starting transfers between devices: 14.7 us -> 22.6 us
  local copies, waits for them, and re-layouts: 3.29 us -> 0.02 us
  other arithmetic: 3.16 us -> 0.27 us
    reduce_scatter x1 -> x0, waiting for transfers between devices: 39.2 us -> none  [body(): lax.psum_scatter(contract_first(combined, pre_grad), 'dev', scatter_dimen...]
    psum x1 -> x0, waiting for transfers between devices: 37.9 us -> none  [body(): weight_grad = lax.psum(weight_shard, 'grp')]
    ppermute x0 -> x17, waiting for transfers between devices: none -> 34.9 us  [permute(): return lax.ppermute(value, AXES, pairs)]
    dot_general x10 -> x0, matrix products: 27.3 us -> none  [the longest x4 9.77 us: contract_first(): lax.dot_general(left_side, right_side, (((0,), (0,)), ((), ())), precisio...]
    ppermute x0 -> x17, starting transfers between devices: none -> 22.6 us  [permute(): return lax.ppermute(value, AXES, pairs)]
    pallas_call x0 -> x11, Pallas kernels: none -> 16.3 us  [the longest x1 3.58 us: body(): back(me, local_adj, mask, inverse, high, low, *grads, *returned)]
    all_to_all x3 -> x0, starting transfers between devices: 14.6 us -> none  [the longest x1 6.35 us: body(): lax.all_to_all(slot_counts, 'grp', split_axis=0, concat_axis=0, tiled=True)]
    all_to_all x3 -> x0, waiting for transfers between devices: 4.59 us -> none  [the longest x1 4.45 us: body(): lax.all_to_all(outgoing.reshape(groups, slot_width, outgoing.shape[1]), '...]
  transfers between devices with their start and end apart: 5 -> 17, of which waited for: 4 -> 9; matrix products, arithmetic and copies ran while one was open for 12% -> 0% of each run, Pallas kernels for 0% -> 17%
where the time goes in v1:
time: 75 us; the launch traced here: 74.9 us
  waiting for transfers between devices  34.9 us (47%)
  starting transfers between devices  22.6 us (30%)
  Pallas kernels  16.3 us (22%)
  between operations  0.79 us (1%)
    ppermute x17, waiting for transfers between devices, permute(): return lax.ppermute(value, AXES, pairs)  34.9 us
    ppermute x17, starting transfers between devices, permute(): return lax.ppermute(value, AXES, pairs)  22.6 us
    pallas_call x1, Pallas kernels, body(): back(me, local_adj, mask, inverse, high, low, *grads, *returned)  3.58 us
    pallas_call x1, Pallas kernels, body(): call(functools.partial(local_kernel, pieces), [shape((nodes, lanes), F32)...  2.66 us
    pallas_call x2, Pallas kernels, body(): call(functools.partial(forward_kernel, edges[c]), [shape((nodes, piece),...  2.35 us
    pallas_call x2, Pallas kernels, body(): call(functools.partial(term_kernel, pair), [shape((block, piece), F32)] *...  1.99 us
    pallas_call x1, Pallas kernels, body(): call(functools.partial(aggregate_kernel, groups, share, orders), [shape((...  1.67 us
  transfers between devices with their start and end apart: 17, of which 9 were waited for; matrix products, arithmetic and copies ran while one was open for 0% of the time, Pallas kernels for 17%

profile of v1, /device:TPU:0, one launch (start us, length us, event | category | flops | bytes accessed | tf_op | source)
XLA Modules:
  0.0 74.9 jit_solution(17646173919062435034)
XLA Ops:
  0.6 1.5 %shard_map.86 = (f32[8,1152]{1,0:T(8,128)S(1)}, f32[8,1152]{1,0:T(8,128)S(1)}, f32[8,1152]{1,0:T(8,128)S(1)}, f32[8,1152]{1,0:T(8,128)S(1)}) custom-call(s32[1]{0:T(128)} %bitcast.me_ref.grp_ref, bf16[256,1024]{1,0:T(8,128)(2,1)} %feats_hbm.3, s32[32,256]{1,0:T(8,128)} %bitcast.4), custom_call_target="tpu_custom_call" | custom-call | flops 16777216 | bytes 557056 | tf_op jit(solution)/shard_map/pallas_call | solution.py:306
  2.1 3.1 %collective-permute-start = (f32[8,1152]{1,0:T(8,128)S(1)}, f32[8,1152]{1,0:T(8,128)S(1)}, u32[]{:S(2)}, u32[]{:S(2)}) collective-permute-start(f32[8,1152]{1,0:T(8,128)S(1)} %get-tuple-element.32), channel_id=1, source_target_pairs={{0,8},{1,9},{2,10},{3,11},{4,12},{5,13},{6,14},{7,15},{8,16},{9,17... | collective-permute-start | bytes 110600 | tf_op jit(solution)/shard_map/ppermute | solution.py:273
  5.2 2.6 %collective-permute-start.1 = (f32[8,1152]{1,0:T(8,128)S(1)}, f32[8,1152]{1,0:T(8,128)S(1)}, u32[]{:S(2)}, u32[]{:S(2)}) collective-permute-start(f32[8,1152]{1,0:T(8,128)S(1)} %get-tuple-element.33), channel_id=1, source_target_pairs={{0,16},{1,17},{2,18},{3,19},{4,20},{5,21},{6,22},{7,23},{8,24},{9,... | collective-permute-start | bytes 110600 | tf_op jit(solution)/shard_map/ppermute | solution.py:273
  7.8 1.3 %collective-permute-start.2 = (f32[8,1152]{1,0:T(8,128)S(1)}, f32[8,1152]{1,0:T(8,128)S(1)}, u32[]{:S(2)}, u32[]{:S(2)}) collective-permute-start(f32[8,1152]{1,0:T(8,128)S(1)} %get-tuple-element.34), channel_id=1, source_target_pairs={{0,24},{1,25},{2,26},{3,27},{4,28},{5,29},{6,30},{7,31},{8,0},{9,1... | collective-permute-start | bytes 110600 | tf_op jit(solution)/shard_map/ppermute | solution.py:273
  9.1 0.0 copy-start.3
  9.1 0.0 copy-start
  9.1 2.7 %shard_map.85 = (f32[256,1024]{1,0:T(8,128)S(1)}, f32[256,128]{1,0:T(8,128)S(1)}, bf16[1024,1024]{1,0:T(8,128)(2,1)S(1)}, bf16[1024,1024]{1,0:T(8,128)(2,1)S(1)}) custom-call(bf16[256,1024]{1,0:T(8,128)(2,1)} %feats_hbm.3, s32[256,256]{1,0:T(8,128)} %adj_ref.1, f32[1024,1024]{1,0:T(8,128)} %weight_hbm.1), custom_call_target="tpu_custom_call" | custom-call | flops 134217728 | bytes 9961472 | tf_op jit(solution)/shard_map/pallas_call | solution.py:322
  11.8 0.0 collective-permute-done.refs_1_
  11.8 0.0 collective-permute-done.1.refs_2_
  11.8 0.0 collective-permute-done.2.refs_3_
  11.8 0.0 copy-done.3
  11.8 1.7 %shard_map.87 = (f32[256,1024]{1,0:T(8,128)S(1)}, f32[256,128]{1,0:T(8,128)S(1)}, bf16[32,256]{1,0:T(8,128)(2,1)S(1)}, f32[512,256]{1,0:T(8,128)S(1)}, f32[512,256]{1,0:T(8,128)S(1)}) custom-call(s32[1]{0:T(128)} %bitcast.me_ref.grp_ref, s32[1]{0:T(128)} %bitcast.1.dev_ref, s32[4,8]{1,0:T(4,128)S(1)} %bitcast.6, f32[256,1024]{1,0:T(8,128)S(1)} %get-tuple-element.29.base_ref, ...), custom_call_target="tpu_custom_call" | custom-call | flops 33554432 | bytes 4194304 | tf_op jit(solution)/shard_map/pallas_call | solution.py:336
  13.5 0.1 collective-permute-start.6
  13.6 0.0 copy-done
  13.6 1.2 %shard_map.88 = (bf16[256,512]{1,0:T(8,128)(2,1)S(1)}, f32[256,512]{1,0:T(8,128)S(1)}) custom-call(f32[256,1024]{1,0:T(8,128)S(1)} %get-tuple-element.37.agg_ref, bf16[1024,1024]{1,0:T(8,128)(2,1)S(1)} %get-tuple-element.38.high_ref, bf16[1024,1024]{1,0:T(8,128)(2,1)S(1)} %get-tuple-element.39.low_ref, bf16[256,1024]{1,0:T(8,128)(2,1)S(1)} %copy-done), custom_call_target="tpu_custom_call" | custom-call | flops 805306368 | bytes 3145728 | tf_op jit(solution)/shard_map/pallas_call | solution.py:361
  14.8 0.6 collective-permute-start.12
  15.4 1.2 %shard_map.89 = (bf16[256,512]{1,0:T(8,128)(2,1)S(1)}, f32[256,512]{1,0:T(8,128)S(1)}) custom-call(f32[256,1024]{1,0:T(8,128)S(1)} %get-tuple-element.37.agg_ref, bf16[1024,1024]{1,0:T(8,128)(2,1)S(1)} %get-tuple-element.38.high_ref, bf16[1024,1024]{1,0:T(8,128)(2,1)S(1)} %get-tuple-element.39.low_ref, bf16[256,1024]{1,0:T(8,128)(2,1)S(1)} %copy-done), custom_call_target="tpu_custom_call" | custom-call | flops 805306368 | bytes 3145728 | tf_op jit(solution)/shard_map/pallas_call | solution.py:361
  16.5 0.1 collective-permute-start.7
  16.6 0.0 collective-permute-done.6.refs_1_
  16.6 0.3 collective-permute-done.12.refs_3_
  16.9 1.0 %shard_map.93 = (f32[256,512]{1,0:T(8,128)S(1)}, f32[256,512]{1,0:T(8,128)S(1)}) custom-call(f32[512,256]{1,0:T(8,128)S(1)} %get-tuple-element.49.refs_0_, f32[512,256]{1,0:T(8,128)S(1)} %collective-permute-done.6.refs_1_, f32[256,512]{1,0:T(8,128)S(1)} %get-tuple-element.40.refs_0_.refs_2_, f32[256,512]{1,0:T(8,128)S(1)} %collective-permute-done.12.refs_3_), custom_call_target="tpu_custom_call" | custom-call | flops 805306368 | bytes 3145728 | tf_op jit(solution)/shard_map/pallas_call | solution.py:373
  17.9 1.6 %collective-permute-start.13 = (f32[256,512]{1,0:T(8,128)S(1)}, f32[256,512]{1,0:T(8,128)S(1)}, u32[]{:S(2)}, u32[]{:S(2)}) collective-permute-start(f32[256,512]{1,0:T(8,128)S(1)} %get-tuple-element.54), channel_id=1, source_target_pairs={{0,2},{1,5},{2,0},{3,7},{4,6},{5,1},{6,4},{7,3},{8,10},{9,13},{10,... | collective-permute-start | bytes 1572872 | tf_op jit(solution)/shard_map/ppermute | solution.py:273
  19.4 0.0 collective-permute-done.7.refs_3_
  19.4 1.0 %shard_map.92 = (f32[256,512]{1,0:T(8,128)S(1)}, f32[256,512]{1,0:T(8,128)S(1)}) custom-call(f32[512,256]{1,0:T(8,128)S(1)} %get-tuple-element.49.refs_0_, f32[512,256]{1,0:T(8,128)S(1)} %collective-permute-done.6.refs_1_, f32[256,512]{1,0:T(8,128)S(1)} %get-tuple-element.41.refs_1_.refs_2_, f32[256,512]{1,0:T(8,128)S(1)} %collective-permute-done.7.refs_3_), custom_call_target="tpu_custom_call" | custom-call | flops 805306368 | bytes 3145728 | tf_op jit(solution)/shard_map/pallas_call | solution.py:373
  20.5 0.6 collective-permute-start.8
  21.1 6.1 %collective-permute-done.13 = f32[256,512]{1,0:T(8,128)S(1)} collective-permute-done((f32[256,512]{1,0:T(8,128)S(1)}, f32[256,512]{1,0:T(8,128)S(1)}, u32[]{:S(2)}, u32[]{:S(2)}) %collective-permute-start.13) | collective-permute-done | bytes 524320 | tf_op jit(solution)/shard_map/ppermute | solution.py:273
  27.2 1.6 %collective-permute-start.14 = (f32[128,512]{1,0:T(8,128)S(1)}, f32[128,512]{1,0:T(8,128)S(1)}, u32[]{:S(2)}, u32[]{:S(2)}) collective-permute-start(f32[128,512]{1,0:T(8,128)S(1)} %slice_add_fusion), channel_id=1, source_target_pairs={{0,4},{1,3},{2,6},{3,1},{4,0},{5,7},{6,2},{7,5},{8,12},{9,11},{10,... | collective-permute-start | bytes 786440 | tf_op jit(solution)/shard_map/ppermute | solution.py:273
  28.8 6.8 %collective-permute-done.8 = f32[256,512]{1,0:T(8,128)S(1)} collective-permute-done((f32[256,512]{1,0:T(8,128)S(1)}, f32[256,512]{1,0:T(8,128)S(1)}, u32[]{:S(2)}, u32[]{:S(2)}) %collective-permute-start.8) | collective-permute-done | bytes 524320 | tf_op jit(solution)/shard_map/ppermute | solution.py:273
  35.6 1.6 %collective-permute-start.9 = (f32[128,512]{1,0:T(8,128)S(1)}, f32[128,512]{1,0:T(8,128)S(1)}, u32[]{:S(2)}, u32[]{:S(2)}) collective-permute-start(f32[128,512]{1,0:T(8,128)S(1)} %slice_add_fusion.2), channel_id=1, source_target_pairs={{0,4},{1,3},{2,6},{3,1},{4,0},{5,7},{6,2},{7,5},{8,12},{9,11},{10,... | collective-permute-start | bytes 786440 | tf_op jit(solution)/shard_map/ppermute | solution.py:273
  37.2 0.0 collective-permute-done.14
  37.2 0.1 fusion
  37.3 0.0 copy-start.1
  37.3 0.0 copy-start.2
  37.3 0.7 collective-permute-start.15
  38.0 4.0 %collective-permute-done.9 = f32[128,512]{1,0:T(8,128)S(1)} collective-permute-done((f32[128,512]{1,0:T(8,128)S(1)}, f32[128,512]{1,0:T(8,128)S(1)}, u32[]{:S(2)}, u32[]{:S(2)}) %collective-permute-start.9) | collective-permute-done | bytes 262176 | tf_op jit(solution)/shard_map/ppermute | solution.py:273
  42.0 0.1 fusion.1
  42.1 0.7 collective-permute-start.10
  42.8 3.5 %collective-permute-done.15 = f32[128,512]{1,0:T(8,128)S(1)} collective-permute-done((f32[128,512]{1,0:T(8,128)S(1)}, f32[128,512]{1,0:T(8,128)S(1)}, u32[]{:S(2)}, u32[]{:S(2)}) %collective-permute-start.15) | collective-permute-done | bytes 262176 | tf_op jit(solution)/shard_map/ppermute | solution.py:273
  46.4 1.5 %collective-permute-start.16 = (f32[128,512]{1,0:T(8,128)S(1)}, f32[128,512]{1,0:T(8,128)S(1)}, u32[]{:S(2)}, u32[]{:S(2)}) collective-permute-start(f32[128,512]{1,0:T(8,128)S(1)} %add.31.total_ref), channel_id=1, source_target_pairs={{0,16},{1,9},{2,18},{3,11},{4,20},{5,13},{6,22},{7,15},{8,24},{9,1... | collective-permute-start | bytes 786440 | tf_op jit(solution)/shard_map/ppermute | solution.py:273
  47.8 8.6 %collective-permute-done.10 = f32[128,512]{1,0:T(8,128)S(1)} collective-permute-done((f32[128,512]{1,0:T(8,128)S(1)}, f32[128,512]{1,0:T(8,128)S(1)}, u32[]{:S(2)}, u32[]{:S(2)}) %collective-permute-start.10) | collective-permute-done | bytes 262176 | tf_op jit(solution)/shard_map/ppermute | solution.py:273
  56.5 1.6 %collective-permute-start.11 = (f32[128,512]{1,0:T(8,128)S(1)}, f32[128,512]{1,0:T(8,128)S(1)}, u32[]{:S(2)}, u32[]{:S(2)}) collective-permute-start(f32[128,512]{1,0:T(8,128)S(1)} %add.27.total_ref), channel_id=1, source_target_pairs={{0,16},{1,9},{2,18},{3,11},{4,20},{5,13},{6,22},{7,15},{8,24},{9,1... | collective-permute-start | bytes 786440 | tf_op jit(solution)/shard_map/ppermute | solution.py:273
  58.1 1.1 %shard_map.90 = (f32[8,1024]{1,0:T(8,128)S(1)}, f32[8,1024]{1,0:T(8,128)S(1)}, f32[8,1024]{1,0:T(8,128)S(1)}, f32[8,1024]{1,0:T(8,128)S(1)}, bf16[256,1024]{1,0:T(8,128)(2,1)}) custom-call(bf16[32,256]{1,0:T(8,128)(2,1)S(1)} %get-tuple-element.35.hot_ref, f32[256,128]{1,0:T(8,128)S(1)} %get-tuple-element.36.inverse_ref, ...), custom_call_target="tpu_custom_call" | custom-call | flops 33554432 | bytes 1048576 | tf_op jit(solution)/shard_map/pallas_call | solution.py:412
  59.2 2.9 %collective-permute-start.3 = (f32[8,1024]{1,0:T(8,128)S(1)}, f32[8,1024]{1,0:T(8,128)S(1)}, u32[]{:S(2)}, u32[]{:S(2)}) collective-permute-start(f32[8,1024]{1,0:T(8,128)S(1)} %get-tuple-element.46), channel_id=1, source_target_pairs={{0,24},{1,25},{2,26},{3,27},{4,28},{5,29},{6,30},{7,31},{8,0},{9,1... | collective-permute-start | bytes 98312 | tf_op jit(solution)/shard_map/ppermute | solution.py:273
  62.1 2.0 %collective-permute-start.4 = (f32[8,1024]{1,0:T(8,128)S(1)}, f32[8,1024]{1,0:T(8,128)S(1)}, u32[]{:S(2)}, u32[]{:S(2)}) collective-permute-start(f32[8,1024]{1,0:T(8,128)S(1)} %get-tuple-element.47), channel_id=1, source_target_pairs={{0,16},{1,17},{2,18},{3,19},{4,20},{5,21},{6,22},{7,23},{8,24},{9,... | collective-permute-start | bytes 98312 | tf_op jit(solution)/shard_map/ppermute | solution.py:273
  64.1 0.0 collective-permute-start.5
  64.1 0.4 collective-permute-done.3.refs_3_
  64.5 3.2 %collective-permute-done.4.refs_4_ = f32[8,1024]{1,0:T(8,128)S(1)} collective-permute-done((f32[8,1024]{1,0:T(8,128)S(1)}, f32[8,1024]{1,0:T(8,128)S(1)}, u32[]{:S(2)}, u32[]{:S(2)}) %collective-permute-start.4) | collective-permute-done | bytes 32800 | tf_op jit(solution)/shard_map/ppermute | solution.py:273
  67.7 2.1 %collective-permute-done.5.refs_5_ = f32[8,1024]{1,0:T(8,128)S(1)} collective-permute-done((f32[8,1024]{1,0:T(8,128)S(1)}, f32[8,1024]{1,0:T(8,128)S(1)}, u32[]{:S(2)}, u32[]{:S(2)}) %collective-permute-start.5) | collective-permute-done | bytes 32800 | tf_op jit(solution)/shard_map/ppermute | solution.py:273
  69.8 0.0 copy-done.1
  69.8 0.0 copy-done.2
  69.8 3.6 %shard_map.91 = f32[256,1024]{1,0:T(8,128)} custom-call(s32[1]{0:T(128)} %bitcast.me_ref.grp_ref, s32[256,256]{1,0:T(8,128)S(1)} %copy-done.1, s32[32,256]{1,0:T(8,128)S(1)} %bitcast.5, f32[256,128]{1,0:T(8,128)S(1)} %get-tuple-element.36.inverse_ref, bf16[1024,1024]{1,0:T(8,128)(2,1)S(1)} %get-tuple-element.38.high_ref, ...), custom_call_target="tpu_custom_call" | custom-call | flops 1610612736 | bytes 6291456 | tf_op jit(solution)/shard_map/pallas_call | solution.py:450
  73.4 0.0 collective-permute-done.16.refs_0_
  73.4 0.7 shard_map.94.refs_1_
  74.1 0.0 collective-permute-done.11.refs_0_
  74.2 0.7 shard_map.95
  (4 shorter events, 0.2 us)
Async XLA Ops:
  2.1 9.7 %collective-permute-start = (f32[8,1152]{1,0:T(8,128)S(1)}, f32[8,1152]{1,0:T(8,128)S(1)}, u32[]{:S(2)}, u32[]{:S(2)}) collective-permute-start(f32[8,1152]{1,0:T(8,128)S(1)} %get-tuple-element.32), channel_id=1, source_target_pairs={{0,8},{1,9},{2,10},{3,11},{4,12},{5,13},{6,14},{7,15},{8,16},{9,17... | collective-permute-start | bytes 110600 | tf_op jit(solution)/shard_map/ppermute | solution.py:273
  5.2 6.6 %collective-permute-start.1 = (f32[8,1152]{1,0:T(8,128)S(1)}, f32[8,1152]{1,0:T(8,128)S(1)}, u32[]{:S(2)}, u32[]{:S(2)}) collective-permute-start(f32[8,1152]{1,0:T(8,128)S(1)} %get-tuple-element.33), channel_id=1, source_target_pairs={{0,16},{1,17},{2,18},{3,19},{4,20},{5,21},{6,22},{7,23},{8,24},{9,... | collective-permute-start | bytes 110600 | tf_op jit(solution)/shard_map/ppermute | solution.py:273
  7.8 4.0 %collective-permute-start.2 = (f32[8,1152]{1,0:T(8,128)S(1)}, f32[8,1152]{1,0:T(8,128)S(1)}, u32[]{:S(2)}, u32[]{:S(2)}) collective-permute-start(f32[8,1152]{1,0:T(8,128)S(1)} %get-tuple-element.34), channel_id=1, source_target_pairs={{0,24},{1,25},{2,26},{3,27},{4,28},{5,29},{6,30},{7,31},{8,0},{9,1... | collective-permute-start | bytes 110600 | tf_op jit(solution)/shard_map/ppermute | solution.py:273
  9.1 2.7 %copy-start.3 = (s32[1,1,4,8]{3,2,1,0:T(4,128)S(1)}, s32[1,1,4,8]{3,2,1,0:T(4,128)}, u32[]{:S(2)}) copy-start(s32[1,1,4,8]{3,2,1,0:T(4,128)} %param.11) | copy-start | bytes 388
  9.1 4.5 %copy-start = (bf16[256,1024]{1,0:T(8,128)(2,1)S(1)}, bf16[256,1024]{1,0:T(8,128)(2,1)}, u32[]{:S(2)}) copy-start(bf16[256,1024]{1,0:T(8,128)(2,1)} %cot_ref.3) | copy-start | bytes 1572868
  13.5 3.1 %collective-permute-start.6 = (f32[512,256]{1,0:T(8,128)S(1)}, f32[512,256]{1,0:T(8,128)S(1)}, u32[]{:S(2)}, u32[]{:S(2)}) collective-permute-start(f32[512,256]{1,0:T(8,128)S(1)} %get-tuple-element.50), channel_id=1, source_target_pairs={{0,1},{1,0},{2,3},{3,2},{4,5},{5,4},{6,7},{7,6},{8,9},{9,8},{10,11... | collective-permute-start | bytes 1572872 | tf_op jit(solution)/shard_map/ppermute | solution.py:273
  14.8 2.1 %collective-permute-start.12 = (f32[256,512]{1,0:T(8,128)S(1)}, f32[256,512]{1,0:T(8,128)S(1)}, u32[]{:S(2)}, u32[]{:S(2)}) collective-permute-start(f32[256,512]{1,0:T(8,128)S(1)} %get-tuple-element.40.refs_0_.refs_2_), channel_id=1, source_target_pairs={{0,1},{1,0},{2,3},{3,2},{4,5},{5,4},{6,7},{7,6},{8,9},{9,8},{10,11... | collective-permute-start | bytes 1572872 | tf_op jit(solution)/shard_map/ppermute | solution.py:273
  16.5 2.9 %collective-permute-start.7 = (f32[256,512]{1,0:T(8,128)S(1)}, f32[256,512]{1,0:T(8,128)S(1)}, u32[]{:S(2)}, u32[]{:S(2)}) collective-permute-start(f32[256,512]{1,0:T(8,128)S(1)} %get-tuple-element.41.refs_1_.refs_2_), channel_id=1, source_target_pairs={{0,1},{1,0},{2,3},{3,2},{4,5},{5,4},{6,7},{7,6},{8,9},{9,8},{10,11... | collective-permute-start | bytes 1572872 | tf_op jit(solution)/shard_map/ppermute | solution.py:273
  17.9 9.2 %collective-permute-start.13 = (f32[256,512]{1,0:T(8,128)S(1)}, f32[256,512]{1,0:T(8,128)S(1)}, u32[]{:S(2)}, u32[]{:S(2)}) collective-permute-start(f32[256,512]{1,0:T(8,128)S(1)} %get-tuple-element.54), channel_id=1, source_target_pairs={{0,2},{1,5},{2,0},{3,7},{4,6},{5,1},{6,4},{7,3},{8,10},{9,13},{10,... | collective-permute-start | bytes 1572872 | tf_op jit(solution)/shard_map/ppermute | solution.py:273
  20.5 15.1 %collective-permute-start.8 = (f32[256,512]{1,0:T(8,128)S(1)}, f32[256,512]{1,0:T(8,128)S(1)}, u32[]{:S(2)}, u32[]{:S(2)}) collective-permute-start(f32[256,512]{1,0:T(8,128)S(1)} %get-tuple-element.52), channel_id=1, source_target_pairs={{0,2},{1,5},{2,0},{3,7},{4,6},{5,1},{6,4},{7,3},{8,10},{9,13},{10,... | collective-permute-start | bytes 1572872 | tf_op jit(solution)/shard_map/ppermute | solution.py:273
  27.2 10.0 %collective-permute-start.14 = (f32[128,512]{1,0:T(8,128)S(1)}, f32[128,512]{1,0:T(8,128)S(1)}, u32[]{:S(2)}, u32[]{:S(2)}) collective-permute-start(f32[128,512]{1,0:T(8,128)S(1)} %slice_add_fusion), channel_id=1, source_target_pairs={{0,4},{1,3},{2,6},{3,1},{4,0},{5,7},{6,2},{7,5},{8,12},{9,11},{10,... | collective-permute-start | bytes 786440 | tf_op jit(solution)/shard_map/ppermute | solution.py:273
  35.6 6.4 %collective-permute-start.9 = (f32[128,512]{1,0:T(8,128)S(1)}, f32[128,512]{1,0:T(8,128)S(1)}, u32[]{:S(2)}, u32[]{:S(2)}) collective-permute-start(f32[128,512]{1,0:T(8,128)S(1)} %slice_add_fusion.2), channel_id=1, source_target_pairs={{0,4},{1,3},{2,6},{3,1},{4,0},{5,7},{6,2},{7,5},{8,12},{9,11},{10,... | collective-permute-start | bytes 786440 | tf_op jit(solution)/shard_map/ppermute | solution.py:273
  37.3 32.6 %copy-start.1 = (s32[256,256]{1,0:T(8,128)S(1)}, s32[256,256]{1,0:T(8,128)}, u32[]{:S(2)}) copy-start(s32[256,256]{1,0:T(8,128)} %adj_ref.1) | copy-start | bytes 786436
  37.3 32.5 %copy-start.2 = (s32[1,1,4,8,256]{4,3,2,1,0:T(8,128)S(1)}, s32[1,1,4,8,256]{4,3,2,1,0:T(8,128)}, u32[]{:S(2)}) copy-start(s32[1,1,4,8,256]{4,3,2,1,0:T(8,128)} %param.10) | copy-start | bytes 98308
  37.3 9.0 %collective-permute-start.15 = (f32[128,512]{1,0:T(8,128)S(1)}, f32[128,512]{1,0:T(8,128)S(1)}, u32[]{:S(2)}, u32[]{:S(2)}) collective-permute-start(f32[128,512]{1,0:T(8,128)S(1)} %fusion), channel_id=1, source_target_pairs={{0,8},{1,17},{2,10},{3,19},{4,12},{5,21},{6,14},{7,23},{8,0},{9,25... | collective-permute-start | bytes 786440 | tf_op jit(solution)/shard_map/ppermute | solution.py:273
  42.1 14.4 %collective-permute-start.10 = (f32[128,512]{1,0:T(8,128)S(1)}, f32[128,512]{1,0:T(8,128)S(1)}, u32[]{:S(2)}, u32[]{:S(2)}) collective-permute-start(f32[128,512]{1,0:T(8,128)S(1)} %fusion.1), channel_id=1, source_target_pairs={{0,8},{1,17},{2,10},{3,19},{4,12},{5,21},{6,14},{7,23},{8,0},{9,25... | collective-permute-start | bytes 786440 | tf_op jit(solution)/shard_map/ppermute | solution.py:273
  46.4 27.0 %collective-permute-start.16 = (f32[128,512]{1,0:T(8,128)S(1)}, f32[128,512]{1,0:T(8,128)S(1)}, u32[]{:S(2)}, u32[]{:S(2)}) collective-permute-start(f32[128,512]{1,0:T(8,128)S(1)} %add.31.total_ref), channel_id=1, source_target_pairs={{0,16},{1,9},{2,18},{3,11},{4,20},{5,13},{6,22},{7,15},{8,24},{9,1... | collective-permute-start | bytes 786440 | tf_op jit(solution)/shard_map/ppermute | solution.py:273
  56.5 17.6 %collective-permute-start.11 = (f32[128,512]{1,0:T(8,128)S(1)}, f32[128,512]{1,0:T(8,128)S(1)}, u32[]{:S(2)}, u32[]{:S(2)}) collective-permute-start(f32[128,512]{1,0:T(8,128)S(1)} %add.27.total_ref), channel_id=1, source_target_pairs={{0,16},{1,9},{2,18},{3,11},{4,20},{5,13},{6,22},{7,15},{8,24},{9,1... | collective-permute-start | bytes 786440 | tf_op jit(solution)/shard_map/ppermute | solution.py:273
  59.2 5.3 %collective-permute-start.3 = (f32[8,1024]{1,0:T(8,128)S(1)}, f32[8,1024]{1,0:T(8,128)S(1)}, u32[]{:S(2)}, u32[]{:S(2)}) collective-permute-start(f32[8,1024]{1,0:T(8,128)S(1)} %get-tuple-element.46), channel_id=1, source_target_pairs={{0,24},{1,25},{2,26},{3,27},{4,28},{5,29},{6,30},{7,31},{8,0},{9,1... | collective-permute-start | bytes 98312 | tf_op jit(solution)/shard_map/ppermute | solution.py:273
  62.1 5.7 %collective-permute-start.4 = (f32[8,1024]{1,0:T(8,128)S(1)}, f32[8,1024]{1,0:T(8,128)S(1)}, u32[]{:S(2)}, u32[]{:S(2)}) collective-permute-start(f32[8,1024]{1,0:T(8,128)S(1)} %get-tuple-element.47), channel_id=1, source_target_pairs={{0,16},{1,17},{2,18},{3,19},{4,20},{5,21},{6,22},{7,23},{8,24},{9,... | collective-permute-start | bytes 98312 | tf_op jit(solution)/shard_map/ppermute | solution.py:273
  64.1 5.7 %collective-permute-start.5 = (f32[8,1024]{1,0:T(8,128)S(1)}, f32[8,1024]{1,0:T(8,128)S(1)}, u32[]{:S(2)}, u32[]{:S(2)}) collective-permute-start(f32[8,1024]{1,0:T(8,128)S(1)} %get-tuple-element.48), channel_id=1, source_target_pairs={{0,8},{1,9},{2,10},{3,11},{4,12},{5,13},{6,14},{7,15},{8,16},{9,17... | collective-permute-start | bytes 98312 | tf_op jit(solution)/shard_map/ppermute | solution.py:273

commit v2 on v1

--- a/solution.py
+++ b/solution.py
@@ -12,6 +12,7 @@
 LANES = 128
 EIGHTHS = (4, 4)
 CHUNKS = len(EIGHTHS)
+SHIFTS = ((1, 2), (2, 0))
 LIMIT = 16 << 20
 F32 = jnp.float32
 BF16 = jnp.bfloat16
@@ -150,16 +151,17 @@
     grad_ref[...] = cot_ref[:, at].astype(F32) * slope
 
 
-def term_kernel(count, *refs):
+def term_kernel(count, rows, places, grp_ref, dev_ref, *refs):
     total = None
     for agg_ref, grad_ref in zip(refs[:count], refs[count : 2 * count]):
         part = dot_three(split(agg_ref[...]), split(grad_ref[...]))
         total = part if total is None else total + part
-    outs = refs[2 * count :]
-    start = 0
-    for ref in outs:
-        ref[...] = total[start : start + ref.shape[0]]
-        start += ref.shape[0]
+    outs, total_ref = refs[2 * count : -1], refs[-1]
+    total_ref[...] = total
+    each = outs[0].shape[0] // rows
+    for place, block in enumerate(places(grp_ref[0], dev_ref[0])):
+        ref, at = outs[place // each], place % each * rows
+        ref[at : at + rows, :] = total_ref[pl.ds(pl.multiple_of(block * rows, rows), rows), :]
 
 
 def slots_kernel(width, hot_ref, inverse_ref, *refs):
@@ -177,13 +179,13 @@
         start = stop
 
 
-def last_kernel(start, count, total_ref, *refs):
-    came, (out_ref, sum_ref, sem) = refs[:count], refs[-3:]
-    total = total_ref[...]
-    for ref in came:
-        total = total + ref[...]
-    sum_ref[...] = total
-    columns = pl.ds(start, total.shape[1])
+def last_kernel(start, stage, grp_ref, *refs):
+    pieces, (out_ref, sum_ref, sem) = refs[: stage[1]], refs[-3:]
+    rows = pieces[0].shape[0]
+    for step, ref in enumerate(pieces):
+        digit = lax.rem(lax.div(grp_ref[0], stage[0]) + stage[1] - step, stage[1])
+        sum_ref[pl.ds(pl.multiple_of(digit * rows, rows), rows), :] = ref[...]
+    columns = pl.ds(start, sum_ref.shape[1])
     copy = pltpu.make_async_copy(sum_ref, out_ref.at[:, columns], sem)
     copy.start()
     copy.wait()
@@ -232,14 +234,6 @@
     return stages
 
 
-def turned(stages, shift):
-    run = 0
-    while run < len(stages) and stages[run][1] == stages[0][1]:
-        run += 1
-    shift = shift % run if run else 0
-    return stages[shift:run] + stages[:shift] + stages[run:]
-
-
 def shifted(index, stage, amount):
     stride, factor = stage
     if isinstance(index, int):
@@ -247,6 +241,28 @@
         return index + ((digit + amount) % factor - digit) * stride
     digit = lax.rem(lax.div(index, stride), factor)
     return index + (lax.rem(digit + amount, factor) - digit) * stride
+
+
+def plan(groups, devs):
+    dev_stages, grp_stages = stages_of(devs), stages_of(groups)
+    scatter = [("grp", grp_stages[0])]
+    scatter += [("dev", stage) for stage in reversed(dev_stages[1:])]
+    return dev_stages[0], scatter, grp_stages[1:]
+
+
+def turned(stages, shift):
+    run = 0
+    while run < len(stages) and stages[run][1][1] == stages[0][1][1]:
+        run += 1
+    shift %= run
+    return stages[shift:run] + stages[:shift] + stages[run:]
+
+
+def moved(grp, dev, stage, amount):
+    axis, steps = stage
+    if axis == "grp":
+        return shifted(grp, steps, amount), dev
+    return grp, shifted(dev, steps, amount)
 
 
 def pick(condition_index, values):
@@ -286,21 +302,32 @@
             for d in range(devs)
         ]
 
-    stages = stages_of(devs)
-    first, rest = stages[0], stages[1:]
+    first, scatter, exchange = plan(groups, devs)
     pair = first[1]
-    kinds = [turned(rest, k) for k in range(pair)]
-    grp_kinds = [turned(stages_of(groups), k) for k in range(pair)]
     inner = devs // pair
+    parts = scatter[0][1][1]
+    rows = share // parts
+
+    def kinds(c):
+        return [turned(scatter, SHIFTS[c][digit % 2]) for digit in range(pair)]
 
     def orders(dev, which):
-        dev = shifted(dev, first, which)
+        digit = lax.rem(lax.rem(dev, pair) + which, pair)
+        return [place * pair + digit for place in range(inner)]
+
+    def places(c, grp, dev):
         lists = []
-        for kind in kinds:
-            found = [dev]
+        for kind in kinds(c):
+            found = [(grp, dev)]
             for stage in reversed(kind):
-                found = [shifted(d, stage, e) for e in range(stage[1]) for d in found]
-            lists.append(found)
+                found = [moved(*at, stage, e) for e in range(stage[1][1]) for at in found]
+            lists.append(
+                [
+                    lax.div(d, pair) * parts
+                    + lax.rem(lax.div(g, scatter[0][1][0]), parts)
+                    for g, d in found
+                ]
+            )
         return [pick(lax.rem(dev, pair), same) for same in zip(*lists)]
 
     outgoing = call(
@@ -354,7 +381,7 @@
 
     acts, grads = [], []
     sends, keeps = [], []
-    half = rest[0][1] if rest else 1
+    half = scatter[0][1][1]
     block = inner * share // half
     for c in range(CHUNKS):
         piece = edges[c + 1] - edges[c]
@@ -371,37 +398,46 @@
         piece = edges[c + 1] - edges[c]
         chunk = [grads[c]] + [to_partner(grads[c], k) for k in range(1, pair)]
         outs = call(
-            functools.partial(term_kernel, pair),
+            functools.partial(term_kernel, pair, rows, functools.partial(places, c)),
             [shape((block, piece), F32)] * half,
-            [VMEM] * (2 * pair),
+            [SMEM, SMEM] + [VMEM] * (2 * pair),
             6 * nodes * pair * inner * share * piece,
             inner * share * piece * 4 + nodes * pair * (piece + inner * share) * 4,
-        )(*aggs, *chunk)
+            [pltpu.VMEM((inner * share, piece), F32)],
+        )(me, dev, *aggs, *chunk)
         keeps.append(outs[0])
         sends.append(outs[1:])
 
     totals = []
     for c in range(CHUNKS):
         keep, send = keeps[c], sends[c]
-        for level in range(len(rest)):
-            size = [kind[level][1] for kind in kinds][0]
+        order = kinds(c)
+        for level in range(len(scatter)):
             came = [
                 permute(
-                    send[k - 1], over(lambda g, d, k=k: (g, shifted(d, kinds[d % pair][level], k)))
+                    send[k - 1],
+                    over(lambda g, d, k=k: moved(g, d, order[d % pair][level], k)),
                 )
-                for k in range(1, size)
+                for k in range(1, order[0][level][1][1])
             ]
-            if level + 1 < len(rest):
-                split_in = kinds[0][level + 1][1]
-                step = keep.shape[0] // split_in
-                parts = []
-                for k in range(split_in):
-                    at = slice(k * step, (k + 1) * step)
-                    parts.append(functools.reduce(jnp.add, [keep[at]] + [v[at] for v in came]))
-                keep, send = parts[0], parts[1:]
-            else:
+            if level + 1 == len(scatter):
                 keep = functools.reduce(jnp.add, [keep] + came)
+                continue
+            split_in = order[0][level + 1][1][1]
+            step = keep.shape[0] // split_in
+            halves = []
+            for k in range(split_in):
+                at = slice(k * step, (k + 1) * step)
+                halves.append(functools.reduce(jnp.add, [keep[at]] + [v[at] for v in came]))
+            keep, send = halves[0], halves[1:]
+        for stage in exchange:
+            came = [
+                permute(keep, over(lambda g, d, k=k: (shifted(g, stage, k), d)))
+                for k in range(1, stage[1])
+            ]
+            keep = functools.reduce(jnp.add, [keep] + came)
         totals.append(keep)
+
     pick_slots = call(
         functools.partial(slots_kernel, width),
         [shape((width, outer), F32)] * groups + [shape((nodes, outer), BF16)],
@@ -411,32 +447,24 @@
     )
     *slot_rows, activated = pick_slots(hot, inverse, *grads, *acts)
     weight_grad = None
-    levels = len(grp_kinds[0])
-    for level in range(levels):
-        size = grp_kinds[0][level][1]
-        for c in range(CHUNKS):
-            came = [
-                permute(
-                    totals[c],
-                    over(lambda g, d, k=k: (shifted(g, grp_kinds[d % pair][level], k), d)),
-                )
-                for k in range(1, size)
-            ]
-            if level + 1 < levels:
-                totals[c] = functools.reduce(jnp.add, [totals[c]] + came)
-                continue
-            piece = edges[c + 1] - edges[c]
-            before = [] if weight_grad is None else [weight_grad]
-            weight_grad = call(
-                functools.partial(last_kernel, edges[c], len(came)),
-                shape((share, outer), F32),
-                [VMEM] * (1 + len(came)) + [HBM] * len(before),
-                share * piece,
-                share * piece * 4,
-                [pltpu.VMEM((share, piece), F32), pltpu.SemaphoreType.DMA],
-                HBM,
-                {1 + len(came): 0} if before else None,
-            )(totals[c], *came, *before)
+    for c in range(CHUNKS):
+        stage = scatter[0][1]
+        came = [
+            permute(totals[c], over(lambda g, d, k=k: (shifted(g, stage, k), d)))
+            for k in range(1, stage[1])
+        ]
+        piece = edges[c + 1] - edges[c]
+        before = [] if weight_grad is None else [weight_grad]
+        weight_grad = call(
+            functools.partial(last_kernel, edges[c], stage),
+            shape((share, outer), F32),
+            [SMEM] + [VMEM] * stage[1] + [HBM] * len(before),
+            share * piece,
+            share * piece * 4,
+            [pltpu.VMEM((share, piece), F32), pltpu.SemaphoreType.DMA],
+            HBM,
+            {1 + stage[1]: 0} if before else None,
+        )(me, totals[c], *came, *before)
     returned = [slot_rows[0]] + [
         permute(slot_rows[k], over_grp(groups - k)) for k in range(1, groups)
     ]

time: 75 us -> 66.9 us (0.89)
  waiting for transfers between devices: 34.9 us -> 26.3 us
    ppermute x17 -> x19, waiting for transfers between devices: 34.9 us -> 26.3 us  [permute(): return lax.ppermute(value, AXES, pairs)]
    ppermute x17 -> x19, starting transfers between devices: 22.6 us -> 22.8 us  [permute(): return lax.ppermute(value, AXES, pairs)]
  transfers between devices with their start and end apart: 17 -> 19, of which waited for: 9 -> 8; matrix products, arithmetic and copies ran while one was open for 0% -> 0% of each run, Pallas kernels for 17% -> 19%
where the time goes in v2:
time: 66.9 us; the launch traced here: 66.8 us
  waiting for transfers between devices  26.3 us (39%)
  starting transfers between devices  22.8 us (34%)
  Pallas kernels  16.6 us (25%)
  between operations  0.8 us (1%)
    ppermute x19, waiting for transfers between devices, permute(): return lax.ppermute(value, AXES, pairs)  26.3 us
    ppermute x19, starting transfers between devices, permute(): return lax.ppermute(value, AXES, pairs)  22.8 us
    pallas_call x1, Pallas kernels, body(): back(me, local_adj, mask, inverse, high, low, *grads, *returned)  3.58 us
    pallas_call x1, Pallas kernels, body(): call(functools.partial(local_kernel, pieces), [shape((nodes, lanes), F32)...  2.66 us
    pallas_call x2, Pallas kernels, body(): call(functools.partial(forward_kernel, edges[c]), [shape((nodes, piece),...  2.37 us
    pallas_call x2, Pallas kernels, body(): call(functools.partial(term_kernel, pair, rows, functools.partial(places,...  2.14 us
    pallas_call x1, Pallas kernels, body(): call(functools.partial(aggregate_kernel, groups, share, orders), [shape((...  1.82 us
    pallas_call x2, Pallas kernels, body(): call(functools.partial(last_kernel, edges[c], stage), shape((share, outer...  1.47 us
  transfers between devices with their start and end apart: 19, of which 8 were waited for; matrix products, arithmetic and copies ran while one was open for 0% of the time, Pallas kernels for 19%

profile of v2, /device:TPU:0, one launch (start us, length us, event | category | flops | bytes accessed | tf_op | source)
XLA Modules:
  0.0 66.8 jit_solution(4233572589911737791)
XLA Ops:
  0.6 1.5 %shard_map.86 = (f32[8,1152]{1,0:T(8,128)S(1)}, f32[8,1152]{1,0:T(8,128)S(1)}, f32[8,1152]{1,0:T(8,128)S(1)}, f32[8,1152]{1,0:T(8,128)S(1)}) custom-call(s32[1]{0:T(128)} %bitcast.me_ref.grp_ref, bf16[256,1024]{1,0:T(8,128)(2,1)} %feats_hbm.3, s32[32,256]{1,0:T(8,128)} %bitcast.4), custom_call_target="tpu_custom_call" | custom-call | flops 16777216 | bytes 557056 | tf_op jit(solution)/shard_map/pallas_call | solution.py:333
  2.1 3.1 %collective-permute-start = (f32[8,1152]{1,0:T(8,128)S(1)}, f32[8,1152]{1,0:T(8,128)S(1)}, u32[]{:S(2)}, u32[]{:S(2)}) collective-permute-start(f32[8,1152]{1,0:T(8,128)S(1)} %get-tuple-element.32), channel_id=1, source_target_pairs={{0,8},{1,9},{2,10},{3,11},{4,12},{5,13},{6,14},{7,15},{8,16},{9,17... | collective-permute-start | bytes 110600 | tf_op jit(solution)/shard_map/ppermute | solution.py:289
  5.2 2.6 %collective-permute-start.1 = (f32[8,1152]{1,0:T(8,128)S(1)}, f32[8,1152]{1,0:T(8,128)S(1)}, u32[]{:S(2)}, u32[]{:S(2)}) collective-permute-start(f32[8,1152]{1,0:T(8,128)S(1)} %get-tuple-element.33), channel_id=1, source_target_pairs={{0,16},{1,17},{2,18},{3,19},{4,20},{5,21},{6,22},{7,23},{8,24},{9,... | collective-permute-start | bytes 110600 | tf_op jit(solution)/shard_map/ppermute | solution.py:289
  7.8 1.3 %collective-permute-start.2 = (f32[8,1152]{1,0:T(8,128)S(1)}, f32[8,1152]{1,0:T(8,128)S(1)}, u32[]{:S(2)}, u32[]{:S(2)}) collective-permute-start(f32[8,1152]{1,0:T(8,128)S(1)} %get-tuple-element.34), channel_id=1, source_target_pairs={{0,24},{1,25},{2,26},{3,27},{4,28},{5,29},{6,30},{7,31},{8,0},{9,1... | collective-permute-start | bytes 110600 | tf_op jit(solution)/shard_map/ppermute | solution.py:289
  9.1 0.0 copy-start.3
  9.1 0.0 copy-start
  9.1 2.7 %shard_map.85 = (f32[256,1024]{1,0:T(8,128)S(1)}, f32[256,128]{1,0:T(8,128)S(1)}, bf16[1024,1024]{1,0:T(8,128)(2,1)S(1)}, bf16[1024,1024]{1,0:T(8,128)(2,1)S(1)}) custom-call(bf16[256,1024]{1,0:T(8,128)(2,1)} %feats_hbm.3, s32[256,256]{1,0:T(8,128)} %adj_ref.1, f32[1024,1024]{1,0:T(8,128)} %weight_hbm.1), custom_call_target="tpu_custom_call" | custom-call | flops 134217728 | bytes 9961472 | tf_op jit(solution)/shard_map/pallas_call | solution.py:349
  11.8 0.0 collective-permute-done.refs_1_
  11.8 0.0 collective-permute-done.1.refs_2_
  11.8 0.0 collective-permute-done.2.refs_3_
  11.8 0.0 copy-done.3
  11.8 1.8 %shard_map.87 = (f32[256,1024]{1,0:T(8,128)S(1)}, f32[256,128]{1,0:T(8,128)S(1)}, bf16[32,256]{1,0:T(8,128)(2,1)S(1)}, f32[512,256]{1,0:T(8,128)S(1)}, f32[512,256]{1,0:T(8,128)S(1)}) custom-call(s32[1]{0:T(128)} %bitcast.me_ref.grp_ref, s32[1]{0:T(128)} %bitcast.1.dev_ref, s32[4,8]{1,0:T(4,128)S(1)} %bitcast.6, f32[256,1024]{1,0:T(8,128)S(1)} %get-tuple-element.29.base_ref, ...), custom_call_target="tpu_custom_call" | custom-call | flops 33554432 | bytes 4194304 | tf_op jit(solution)/shard_map/pallas_call | solution.py:363
  13.7 0.1 collective-permute-start.6
  13.7 0.0 copy-done
  13.8 1.2 %shard_map.89 = (bf16[256,512]{1,0:T(8,128)(2,1)S(1)}, f32[256,512]{1,0:T(8,128)S(1)}) custom-call(f32[256,1024]{1,0:T(8,128)S(1)} %get-tuple-element.37.agg_ref, bf16[1024,1024]{1,0:T(8,128)(2,1)S(1)} %get-tuple-element.38.high_ref, bf16[1024,1024]{1,0:T(8,128)(2,1)S(1)} %get-tuple-element.39.low_ref, bf16[256,1024]{1,0:T(8,128)(2,1)S(1)} %copy-done), custom_call_target="tpu_custom_call" | custom-call | flops 805306368 | bytes 3145728 | tf_op jit(solution)/shard_map/pallas_call | solution.py:388
  15.0 0.6 collective-permute-start.7
  15.5 1.2 %shard_map.88 = (bf16[256,512]{1,0:T(8,128)(2,1)S(1)}, f32[256,512]{1,0:T(8,128)S(1)}) custom-call(f32[256,1024]{1,0:T(8,128)S(1)} %get-tuple-element.37.agg_ref, bf16[1024,1024]{1,0:T(8,128)(2,1)S(1)} %get-tuple-element.38.high_ref, bf16[1024,1024]{1,0:T(8,128)(2,1)S(1)} %get-tuple-element.39.low_ref, bf16[256,1024]{1,0:T(8,128)(2,1)S(1)} %copy-done), custom_call_target="tpu_custom_call" | custom-call | flops 805306368 | bytes 3145728 | tf_op jit(solution)/shard_map/pallas_call | solution.py:388
  16.7 0.1 collective-permute-start.13
  16.8 0.0 collective-permute-done.6.refs_1_
  16.8 0.3 collective-permute-done.7.refs_3_
  17.0 1.1 %shard_map.92 = (f32[256,512]{1,0:T(8,128)S(1)}, f32[256,512]{1,0:T(8,128)S(1)}) custom-call(s32[1]{0:T(128)} %bitcast.me_ref.grp_ref, s32[1]{0:T(128)} %bitcast.1.dev_ref, f32[512,256]{1,0:T(8,128)S(1)} %get-tuple-element.49.refs_0_, f32[512,256]{1,0:T(8,128)S(1)} %collective-permute-done.6.refs_1_, f32[256,512]{1,0:T(8,128)S(1)} %get-tuple-element.41.refs_1_.refs_2_, ...), custom_call_target="tpu_custom_call" | custom-call | flops 805306368 | bytes 3145728 | tf_op jit(solution)/shard_map/pallas_call | solution.py:400
  18.1 1.5 %collective-permute-start.8 = (f32[256,512]{1,0:T(8,128)S(1)}, f32[256,512]{1,0:T(8,128)S(1)}, u32[]{:S(2)}, u32[]{:S(2)}) collective-permute-start(f32[256,512]{1,0:T(8,128)S(1)} %get-tuple-element.52), channel_id=1, source_target_pairs={{0,2},{1,9},{2,0},{3,11},{4,6},{5,13},{6,4},{7,15},{8,10},{9,1},{1... | collective-permute-start | bytes 1572872 | tf_op jit(solution)/shard_map/ppermute | solution.py:289
  19.7 0.0 collective-permute-done.13.refs_3_
  19.7 1.1 %shard_map.93 = (f32[256,512]{1,0:T(8,128)S(1)}, f32[256,512]{1,0:T(8,128)S(1)}) custom-call(s32[1]{0:T(128)} %bitcast.me_ref.grp_ref, s32[1]{0:T(128)} %bitcast.1.dev_ref, f32[512,256]{1,0:T(8,128)S(1)} %get-tuple-element.49.refs_0_, f32[512,256]{1,0:T(8,128)S(1)} %collective-permute-done.6.refs_1_, f32[256,512]{1,0:T(8,128)S(1)} %get-tuple-element.40.refs_0_.refs_2_, ...), custom_call_target="tpu_custom_call" | custom-call | flops 805306368 | bytes 3145728 | tf_op jit(solution)/shard_map/pallas_call | solution.py:400
  20.8 1.6 %collective-permute-start.14 = (f32[256,512]{1,0:T(8,128)S(1)}, f32[256,512]{1,0:T(8,128)S(1)}, u32[]{:S(2)}, u32[]{:S(2)}) collective-permute-start(f32[256,512]{1,0:T(8,128)S(1)} %get-tuple-element.54), channel_id=1, source_target_pairs={{0,4},{1,3},{2,6},{3,1},{4,0},{5,7},{6,2},{7,5},{8,12},{9,11},{10,... | collective-permute-start | bytes 1572872 | tf_op jit(solution)/shard_map/ppermute | solution.py:289
  22.3 9.7 %collective-permute-done.8 = f32[256,512]{1,0:T(8,128)S(1)} collective-permute-done((f32[256,512]{1,0:T(8,128)S(1)}, f32[256,512]{1,0:T(8,128)S(1)}, u32[]{:S(2)}, u32[]{:S(2)}) %collective-permute-start.8) | collective-permute-done | bytes 524320 | tf_op jit(solution)/shard_map/ppermute | solution.py:289
  32.0 0.1 slice_add_fusion.3
  32.1 0.1 collective-permute-start.9
  32.2 0.0 collective-permute-done.14
  32.2 0.1 slice_add_fusion.1
  32.3 1.6 %collective-permute-start.15 = (f32[128,512]{1,0:T(8,128)S(1)}, f32[128,512]{1,0:T(8,128)S(1)}, u32[]{:S(2)}, u32[]{:S(2)}) collective-permute-start(f32[128,512]{1,0:T(8,128)S(1)} %get-tuple-element.56), channel_id=1, source_target_pairs={{0,2},{1,9},{2,0},{3,11},{4,6},{5,13},{6,4},{7,15},{8,10},{9,1},{1... | collective-permute-start | bytes 786440 | tf_op jit(solution)/shard_map/ppermute | solution.py:289
  33.9 7.3 %collective-permute-done.9 = f32[128,512]{1,0:T(8,128)S(1)} collective-permute-done((f32[128,512]{1,0:T(8,128)S(1)}, f32[128,512]{1,0:T(8,128)S(1)}, u32[]{:S(2)}, u32[]{:S(2)}) %collective-permute-start.9) | collective-permute-done | bytes 262176 | tf_op jit(solution)/shard_map/ppermute | solution.py:289
  41.2 0.0 copy-start.1
  41.2 0.0 copy-start.2
  41.2 1.6 %collective-permute-start.10 = (f32[64,512]{1,0:T(8,128)S(1)}, f32[64,512]{1,0:T(8,128)S(1)}, u32[]{:S(2)}, u32[]{:S(2)}) collective-permute-start(f32[64,512]{1,0:T(8,128)S(1)} %slice_add_fusion.6), channel_id=1, source_target_pairs={{0,4},{1,3},{2,6},{3,1},{4,0},{5,7},{6,2},{7,5},{8,12},{9,11},{10,... | collective-permute-start | bytes 393224 | tf_op jit(solution)/shard_map/ppermute | solution.py:289
  42.8 0.0 collective-permute-done.15
  42.8 0.1 collective-permute-start.16
  42.9 3.7 %collective-permute-done.10 = f32[64,512]{1,0:T(8,128)S(1)} collective-permute-done((f32[64,512]{1,0:T(8,128)S(1)}, f32[64,512]{1,0:T(8,128)S(1)}, u32[]{:S(2)}, u32[]{:S(2)}) %collective-permute-start.10) | collective-permute-done | bytes 131104 | tf_op jit(solution)/shard_map/ppermute | solution.py:289
  46.6 2.0 %collective-permute-start.11 = (f32[64,512]{1,0:T(8,128)S(1)}, f32[64,512]{1,0:T(8,128)S(1)}, u32[]{:S(2)}, u32[]{:S(2)}) collective-permute-start(f32[64,512]{1,0:T(8,128)S(1)} %fusion.1), channel_id=1, source_target_pairs={{0,16},{1,17},{2,18},{3,19},{4,20},{5,21},{6,22},{7,23},{8,24},{9,... | collective-permute-start | bytes 393224 | tf_op jit(solution)/shard_map/ppermute | solution.py:289
  48.7 0.0 collective-permute-done.16
  48.7 1.5 %collective-permute-start.17 = (f32[64,512]{1,0:T(8,128)S(1)}, f32[64,512]{1,0:T(8,128)S(1)}, u32[]{:S(2)}, u32[]{:S(2)}) collective-permute-start(f32[64,512]{1,0:T(8,128)S(1)} %fusion), channel_id=1, source_target_pairs={{0,16},{1,17},{2,18},{3,19},{4,20},{5,21},{6,22},{7,23},{8,24},{9,... | collective-permute-start | bytes 393224 | tf_op jit(solution)/shard_map/ppermute | solution.py:289
  50.2 1.1 %shard_map.90 = (f32[8,1024]{1,0:T(8,128)S(1)}, f32[8,1024]{1,0:T(8,128)S(1)}, f32[8,1024]{1,0:T(8,128)S(1)}, f32[8,1024]{1,0:T(8,128)S(1)}, bf16[256,1024]{1,0:T(8,128)(2,1)}) custom-call(bf16[32,256]{1,0:T(8,128)(2,1)S(1)} %get-tuple-element.35.hot_ref, f32[256,128]{1,0:T(8,128)S(1)} %get-tuple-element.36.inverse_ref, ...), custom_call_target="tpu_custom_call" | custom-call | flops 33554432 | bytes 1048576 | tf_op jit(solution)/shard_map/pallas_call | solution.py:448
  51.3 2.4 %collective-permute-start.3 = (f32[8,1024]{1,0:T(8,128)S(1)}, f32[8,1024]{1,0:T(8,128)S(1)}, u32[]{:S(2)}, u32[]{:S(2)}) collective-permute-start(f32[8,1024]{1,0:T(8,128)S(1)} %get-tuple-element.46), channel_id=1, source_target_pairs={{0,24},{1,25},{2,26},{3,27},{4,28},{5,29},{6,30},{7,31},{8,0},{9,1... | collective-permute-start | bytes 98312 | tf_op jit(solution)/shard_map/ppermute | solution.py:289
  53.7 1.9 %collective-permute-start.4 = (f32[8,1024]{1,0:T(8,128)S(1)}, f32[8,1024]{1,0:T(8,128)S(1)}, u32[]{:S(2)}, u32[]{:S(2)}) collective-permute-start(f32[8,1024]{1,0:T(8,128)S(1)} %get-tuple-element.47), channel_id=1, source_target_pairs={{0,16},{1,17},{2,18},{3,19},{4,20},{5,21},{6,22},{7,23},{8,24},{9,... | collective-permute-start | bytes 98312 | tf_op jit(solution)/shard_map/ppermute | solution.py:289
  55.6 0.0 collective-permute-start.5
  55.6 1.9 %collective-permute-done.11 = f32[64,512]{1,0:T(8,128)S(1)} collective-permute-done((f32[64,512]{1,0:T(8,128)S(1)}, f32[64,512]{1,0:T(8,128)S(1)}, u32[]{:S(2)}, u32[]{:S(2)}) %collective-permute-start.11) | collective-permute-done | bytes 131104 | tf_op jit(solution)/shard_map/ppermute | solution.py:289
  57.6 0.4 collective-permute-start.12
  58.0 1.4 %collective-permute-done.17 = f32[64,512]{1,0:T(8,128)S(1)} collective-permute-done((f32[64,512]{1,0:T(8,128)S(1)}, f32[64,512]{1,0:T(8,128)S(1)}, u32[]{:S(2)}, u32[]{:S(2)}) %collective-permute-start.17) | collective-permute-done | bytes 131104 | tf_op jit(solution)/shard_map/ppermute | solution.py:289
  59.4 0.3 collective-permute-start.18
  59.8 0.0 collective-permute-done.3.refs_3_
  59.8 0.3 collective-permute-done.4.refs_4_
  60.1 1.6 %collective-permute-done.5.refs_5_ = f32[8,1024]{1,0:T(8,128)S(1)} collective-permute-done((f32[8,1024]{1,0:T(8,128)S(1)}, f32[8,1024]{1,0:T(8,128)S(1)}, u32[]{:S(2)}, u32[]{:S(2)}) %collective-permute-start.5) | collective-permute-done | bytes 32800 | tf_op jit(solution)/shard_map/ppermute | solution.py:289
  61.7 0.0 copy-done.1
  61.7 0.0 copy-done.2
  61.7 3.6 %shard_map.91 = f32[256,1024]{1,0:T(8,128)} custom-call(s32[1]{0:T(128)} %bitcast.me_ref.grp_ref, s32[256,256]{1,0:T(8,128)S(1)} %copy-done.1, s32[32,256]{1,0:T(8,128)S(1)} %bitcast.5, f32[256,128]{1,0:T(8,128)S(1)} %get-tuple-element.36.inverse_ref, bf16[1024,1024]{1,0:T(8,128)(2,1)S(1)} %get-tuple-element.38.high_ref, ...), custom_call_target="tpu_custom_call" | custom-call | flops 1610612736 | bytes 6291456 | tf_op jit(solution)/shard_map/pallas_call | solution.py:478
  65.3 0.0 collective-permute-done.18.refs_1_
  65.3 0.7 %shard_map.94.refs_2_ = f32[128,1024]{1,0:T(8,128)} custom-call(s32[1]{0:T(128)} %bitcast.me_ref.grp_ref, f32[64,512]{1,0:T(8,128)S(1)} %add.47.refs_0_, f32[64,512]{1,0:T(8,128)S(1)} %collective-permute-done.18.refs_1_), custom_call_target="tpu_custom_call" | custom-call | flops 65536 | bytes 262144 | tf_op jit(solution)/shard_map/pallas_call | solution.py:458
  66.0 0.0 collective-permute-done.12.refs_1_
  66.0 0.7 %shard_map.95 = f32[128,1024]{1,0:T(8,128)} custom-call(s32[1]{0:T(128)} %bitcast.me_ref.grp_ref, f32[64,512]{1,0:T(8,128)S(1)} %add.41.refs_0_, f32[64,512]{1,0:T(8,128)S(1)} %collective-permute-done.12.refs_1_, f32[128,1024]{1,0:T(8,128)} %shard_map.94.refs_2_), custom_call_target="tpu_custom_call", output_to_operand_aliasing={{}: (3, {})} | custom-call | flops 65536 | bytes 262144 | tf_op jit(solution)/shard_map/pallas_call | solution.py:458
  (6 shorter events, 0.1 us)
Async XLA Ops:
  2.1 9.7 %collective-permute-start = (f32[8,1152]{1,0:T(8,128)S(1)}, f32[8,1152]{1,0:T(8,128)S(1)}, u32[]{:S(2)}, u32[]{:S(2)}) collective-permute-start(f32[8,1152]{1,0:T(8,128)S(1)} %get-tuple-element.32), channel_id=1, source_target_pairs={{0,8},{1,9},{2,10},{3,11},{4,12},{5,13},{6,14},{7,15},{8,16},{9,17... | collective-permute-start | bytes 110600 | tf_op jit(solution)/shard_map/ppermute | solution.py:289
  5.2 6.6 %collective-permute-start.1 = (f32[8,1152]{1,0:T(8,128)S(1)}, f32[8,1152]{1,0:T(8,128)S(1)}, u32[]{:S(2)}, u32[]{:S(2)}) collective-permute-start(f32[8,1152]{1,0:T(8,128)S(1)} %get-tuple-element.33), channel_id=1, source_target_pairs={{0,16},{1,17},{2,18},{3,19},{4,20},{5,21},{6,22},{7,23},{8,24},{9,... | collective-permute-start | bytes 110600 | tf_op jit(solution)/shard_map/ppermute | solution.py:289
  7.8 4.0 %collective-permute-start.2 = (f32[8,1152]{1,0:T(8,128)S(1)}, f32[8,1152]{1,0:T(8,128)S(1)}, u32[]{:S(2)}, u32[]{:S(2)}) collective-permute-start(f32[8,1152]{1,0:T(8,128)S(1)} %get-tuple-element.34), channel_id=1, source_target_pairs={{0,24},{1,25},{2,26},{3,27},{4,28},{5,29},{6,30},{7,31},{8,0},{9,1... | collective-permute-start | bytes 110600 | tf_op jit(solution)/shard_map/ppermute | solution.py:289
  9.1 2.7 %copy-start.3 = (s32[1,1,4,8]{3,2,1,0:T(4,128)S(1)}, s32[1,1,4,8]{3,2,1,0:T(4,128)}, u32[]{:S(2)}) copy-start(s32[1,1,4,8]{3,2,1,0:T(4,128)} %param.11) | copy-start | bytes 388
  9.1 4.6 %copy-start = (bf16[256,1024]{1,0:T(8,128)(2,1)S(1)}, bf16[256,1024]{1,0:T(8,128)(2,1)}, u32[]{:S(2)}) copy-start(bf16[256,1024]{1,0:T(8,128)(2,1)} %cot_ref.3) | copy-start | bytes 1572868
  13.7 3.1 %collective-permute-start.6 = (f32[512,256]{1,0:T(8,128)S(1)}, f32[512,256]{1,0:T(8,128)S(1)}, u32[]{:S(2)}, u32[]{:S(2)}) collective-permute-start(f32[512,256]{1,0:T(8,128)S(1)} %get-tuple-element.50), channel_id=1, source_target_pairs={{0,1},{1,0},{2,3},{3,2},{4,5},{5,4},{6,7},{7,6},{8,9},{9,8},{10,11... | collective-permute-start | bytes 1572872 | tf_op jit(solution)/shard_map/ppermute | solution.py:289
  15.0 2.1 %collective-permute-start.7 = (f32[256,512]{1,0:T(8,128)S(1)}, f32[256,512]{1,0:T(8,128)S(1)}, u32[]{:S(2)}, u32[]{:S(2)}) collective-permute-start(f32[256,512]{1,0:T(8,128)S(1)} %get-tuple-element.41.refs_1_.refs_2_), channel_id=1, source_target_pairs={{0,1},{1,0},{2,3},{3,2},{4,5},{5,4},{6,7},{7,6},{8,9},{9,8},{10,11... | collective-permute-start | bytes 1572872 | tf_op jit(solution)/shard_map/ppermute | solution.py:289
  16.7 3.0 %collective-permute-start.13 = (f32[256,512]{1,0:T(8,128)S(1)}, f32[256,512]{1,0:T(8,128)S(1)}, u32[]{:S(2)}, u32[]{:S(2)}) collective-permute-start(f32[256,512]{1,0:T(8,128)S(1)} %get-tuple-element.40.refs_0_.refs_2_), channel_id=1, source_target_pairs={{0,1},{1,0},{2,3},{3,2},{4,5},{5,4},{6,7},{7,6},{8,9},{9,8},{10,11... | collective-permute-start | bytes 1572872 | tf_op jit(solution)/shard_map/ppermute | solution.py:289
  18.1 13.9 %collective-permute-start.8 = (f32[256,512]{1,0:T(8,128)S(1)}, f32[256,512]{1,0:T(8,128)S(1)}, u32[]{:S(2)}, u32[]{:S(2)}) collective-permute-start(f32[256,512]{1,0:T(8,128)S(1)} %get-tuple-element.52), channel_id=1, source_target_pairs={{0,2},{1,9},{2,0},{3,11},{4,6},{5,13},{6,4},{7,15},{8,10},{9,1},{1... | collective-permute-start | bytes 1572872 | tf_op jit(solution)/shard_map/ppermute | solution.py:289
  20.8 11.5 %collective-permute-start.14 = (f32[256,512]{1,0:T(8,128)S(1)}, f32[256,512]{1,0:T(8,128)S(1)}, u32[]{:S(2)}, u32[]{:S(2)}) collective-permute-start(f32[256,512]{1,0:T(8,128)S(1)} %get-tuple-element.54), channel_id=1, source_target_pairs={{0,4},{1,3},{2,6},{3,1},{4,0},{5,7},{6,2},{7,5},{8,12},{9,11},{10,... | collective-permute-start | bytes 1572872 | tf_op jit(solution)/shard_map/ppermute | solution.py:289
  32.1 9.1 %collective-permute-start.9 = (f32[128,512]{1,0:T(8,128)S(1)}, f32[128,512]{1,0:T(8,128)S(1)}, u32[]{:S(2)}, u32[]{:S(2)}) collective-permute-start(f32[128,512]{1,0:T(8,128)S(1)} %get-tuple-element.58), channel_id=1, source_target_pairs={{0,8},{1,5},{2,10},{3,7},{4,12},{5,1},{6,14},{7,3},{8,0},{9,13},{1... | collective-permute-start | bytes 786440 | tf_op jit(solution)/shard_map/ppermute | solution.py:289
  32.3 10.5 %collective-permute-start.15 = (f32[128,512]{1,0:T(8,128)S(1)}, f32[128,512]{1,0:T(8,128)S(1)}, u32[]{:S(2)}, u32[]{:S(2)}) collective-permute-start(f32[128,512]{1,0:T(8,128)S(1)} %get-tuple-element.56), channel_id=1, source_target_pairs={{0,2},{1,9},{2,0},{3,11},{4,6},{5,13},{6,4},{7,15},{8,10},{9,1},{1... | collective-permute-start | bytes 786440 | tf_op jit(solution)/shard_map/ppermute | solution.py:289
  41.2 20.5 %copy-start.1 = (s32[256,256]{1,0:T(8,128)S(1)}, s32[256,256]{1,0:T(8,128)}, u32[]{:S(2)}) copy-start(s32[256,256]{1,0:T(8,128)} %adj_ref.1) | copy-start | bytes 786436
  41.2 20.5 %copy-start.2 = (s32[1,1,4,8,256]{4,3,2,1,0:T(8,128)S(1)}, s32[1,1,4,8,256]{4,3,2,1,0:T(8,128)}, u32[]{:S(2)}) copy-start(s32[1,1,4,8,256]{4,3,2,1,0:T(8,128)} %param.10) | copy-start | bytes 98308
  41.2 5.4 %collective-permute-start.10 = (f32[64,512]{1,0:T(8,128)S(1)}, f32[64,512]{1,0:T(8,128)S(1)}, u32[]{:S(2)}, u32[]{:S(2)}) collective-permute-start(f32[64,512]{1,0:T(8,128)S(1)} %slice_add_fusion.6), channel_id=1, source_target_pairs={{0,4},{1,3},{2,6},{3,1},{4,0},{5,7},{6,2},{7,5},{8,12},{9,11},{10,... | collective-permute-start | bytes 393224 | tf_op jit(solution)/shard_map/ppermute | solution.py:289
  42.8 5.8 %collective-permute-start.16 = (f32[64,512]{1,0:T(8,128)S(1)}, f32[64,512]{1,0:T(8,128)S(1)}, u32[]{:S(2)}, u32[]{:S(2)}) collective-permute-start(f32[64,512]{1,0:T(8,128)S(1)} %slice_add_fusion.4), channel_id=1, source_target_pairs={{0,8},{1,5},{2,10},{3,7},{4,12},{5,1},{6,14},{7,3},{8,0},{9,13},{1... | collective-permute-start | bytes 393224 | tf_op jit(solution)/shard_map/ppermute | solution.py:289
  46.6 10.9 %collective-permute-start.11 = (f32[64,512]{1,0:T(8,128)S(1)}, f32[64,512]{1,0:T(8,128)S(1)}, u32[]{:S(2)}, u32[]{:S(2)}) collective-permute-start(f32[64,512]{1,0:T(8,128)S(1)} %fusion.1), channel_id=1, source_target_pairs={{0,16},{1,17},{2,18},{3,19},{4,20},{5,21},{6,22},{7,23},{8,24},{9,... | collective-permute-start | bytes 393224 | tf_op jit(solution)/shard_map/ppermute | solution.py:289
  48.7 10.7 %collective-permute-start.17 = (f32[64,512]{1,0:T(8,128)S(1)}, f32[64,512]{1,0:T(8,128)S(1)}, u32[]{:S(2)}, u32[]{:S(2)}) collective-permute-start(f32[64,512]{1,0:T(8,128)S(1)} %fusion), channel_id=1, source_target_pairs={{0,16},{1,17},{2,18},{3,19},{4,20},{5,21},{6,22},{7,23},{8,24},{9,... | collective-permute-start | bytes 393224 | tf_op jit(solution)/shard_map/ppermute | solution.py:289
  51.3 8.5 %collective-permute-start.3 = (f32[8,1024]{1,0:T(8,128)S(1)}, f32[8,1024]{1,0:T(8,128)S(1)}, u32[]{:S(2)}, u32[]{:S(2)}) collective-permute-start(f32[8,1024]{1,0:T(8,128)S(1)} %get-tuple-element.46), channel_id=1, source_target_pairs={{0,24},{1,25},{2,26},{3,27},{4,28},{5,29},{6,30},{7,31},{8,0},{9,1... | collective-permute-start | bytes 98312 | tf_op jit(solution)/shard_map/ppermute | solution.py:289
  53.7 6.4 %collective-permute-start.4 = (f32[8,1024]{1,0:T(8,128)S(1)}, f32[8,1024]{1,0:T(8,128)S(1)}, u32[]{:S(2)}, u32[]{:S(2)}) collective-permute-start(f32[8,1024]{1,0:T(8,128)S(1)} %get-tuple-element.47), channel_id=1, source_target_pairs={{0,16},{1,17},{2,18},{3,19},{4,20},{5,21},{6,22},{7,23},{8,24},{9,... | collective-permute-start | bytes 98312 | tf_op jit(solution)/shard_map/ppermute | solution.py:289
  55.6 6.1 %collective-permute-start.5 = (f32[8,1024]{1,0:T(8,128)S(1)}, f32[8,1024]{1,0:T(8,128)S(1)}, u32[]{:S(2)}, u32[]{:S(2)}) collective-permute-start(f32[8,1024]{1,0:T(8,128)S(1)} %get-tuple-element.48), channel_id=1, source_target_pairs={{0,8},{1,9},{2,10},{3,11},{4,12},{5,13},{6,14},{7,15},{8,16},{9,17... | collective-permute-start | bytes 98312 | tf_op jit(solution)/shard_map/ppermute | solution.py:289
  57.6 8.4 %collective-permute-start.12 = (f32[64,512]{1,0:T(8,128)S(1)}, f32[64,512]{1,0:T(8,128)S(1)}, u32[]{:S(2)}, u32[]{:S(2)}) collective-permute-start(f32[64,512]{1,0:T(8,128)S(1)} %add.41.refs_0_), channel_id=1, source_target_pairs={{0,8},{1,9},{2,10},{3,11},{4,12},{5,13},{6,14},{7,15},{8,0},{9,1},... | collective-permute-start | bytes 393224 | tf_op jit(solution)/shard_map/ppermute | solution.py:289
  59.4 5.8 %collective-permute-start.18 = (f32[64,512]{1,0:T(8,128)S(1)}, f32[64,512]{1,0:T(8,128)S(1)}, u32[]{:S(2)}, u32[]{:S(2)}) collective-permute-start(f32[64,512]{1,0:T(8,128)S(1)} %add.47.refs_0_), channel_id=1, source_target_pairs={{0,8},{1,9},{2,10},{3,11},{4,12},{5,13},{6,14},{7,15},{8,0},{9,1},... | collective-permute-start | bytes 393224 | tf_op jit(solution)/shard_map/ppermute | solution.py:289

commit v3 on v2

--- a/solution.py
+++ b/solution.py
@@ -114,27 +114,29 @@
         low_ref[rows, :] = low
 
 
-def aggregate_kernel(groups, parts, orders, grp_ref, dev_ref, rows_ref, base_ref, degree_ref, *refs):
-    arrived = jnp.concatenate([ref[...] for ref in refs[:groups]], axis=0)
-    agg_ref, inverse_ref, hot_ref = refs[groups : groups + 3]
-    flipped, turned_ref, flags_ref = refs[groups + 3 : -2], refs[-2], refs[-1]
+def aggregate_kernel(
+    groups, parts, orders, grp_ref, dev_ref, rows_ref, base_ref, degree_ref, *refs
+):
+    arrived, refs = refs[:groups], refs[groups:]
+    agg_high_ref, agg_low_ref, inverse_ref, hot_ref = refs[:4]
+    flipped, (turned_ref, arrived_ref, flags_ref) = refs[4:-3], refs[-3:]
     nodes, lanes = base_ref.shape
-    width = rows_ref.shape[1]
-    index = lax.broadcasted_iota(jnp.int32, (1, nodes), 1)
-    for step in range(groups):
+    width = arrived[0].shape[0]
+    for step, ref in enumerate(arrived):
         source = lax.rem(grp_ref[0] + (groups - step), groups)
-        for slot in range(width):
-            at = step * width + slot
-            flags_ref[at : at + 1, :] = jnp.where(index == rows_ref[source, slot], 1.0, 0.0)
+        arrived_ref[pl.ds(pl.multiple_of(source * width, width), width), :] = ref[...]
+    index = lax.broadcasted_iota(jnp.int32, (nodes, width), 0)
+    for group in range(groups):
+        flags = jnp.where(rows_ref[group : group + 1, :] == index, 1.0, 0.0)
+        flags_ref[:, group * width : (group + 1) * width] = flags
     one_hot = flags_ref[...].astype(BF16)
     hot_ref[...] = one_hot
-    high, low = split(arrived)
-    first = ((0,), (0,))
-    remote = dot(one_hot, high, first) + dot(one_hot, low, first)
+    high, low = split(arrived_ref[...])
+    remote = dot(one_hot, high) + dot(one_hot, low)
     inverse = 1.0 / (1.0 + degree_ref[...] + remote[:, lanes:])
     inverse_ref[...] = inverse
     agg = (base_ref[...] + remote[:, :lanes]) * inverse[:, :1]
-    agg_ref[...] = agg
+    agg_high_ref[...], agg_low_ref[...] = split(agg)
     turned_ref[...] = agg.T
     for which, ref in enumerate(flipped):
         for place, block in enumerate(orders(dev_ref[0], which)):
@@ -142,9 +144,9 @@
             ref[place * parts : (place + 1) * parts, :] = picked
 
 
-def forward_kernel(start, agg_ref, high_ref, low_ref, cot_ref, act_ref, grad_ref):
+def forward_kernel(start, agg_high_ref, agg_low_ref, high_ref, low_ref, cot_ref, act_ref, grad_ref):
     at = slice(start, start + act_ref.shape[1])
-    preact = dot_three(split(agg_ref[...]), (high_ref[:, at], low_ref[:, at]))
+    preact = dot_three((agg_high_ref[...], agg_low_ref[...]), (high_ref[:, at], low_ref[:, at]))
     sigmoid = 1.0 / (1.0 + jnp.exp(-preact))
     act_ref[...] = (preact * sigmoid).astype(BF16)
     slope = sigmoid * (1.0 + preact * (1.0 - sigmoid))
@@ -164,19 +166,21 @@
         ref[at : at + rows, :] = total_ref[pl.ds(pl.multiple_of(block * rows, rows), rows), :]
 
 
-def slots_kernel(width, hot_ref, inverse_ref, *refs):
+def slots_kernel(width, groups, grp_ref, hot_ref, inverse_ref, *refs):
     grads, acts = refs[:CHUNKS], refs[CHUNKS : 2 * CHUNKS]
-    outs, act_ref = refs[2 * CHUNKS : -1], refs[-1]
+    outs, act_ref, rows_ref = refs[2 * CHUNKS : -2], refs[-2], refs[-1]
     one_hot = hot_ref[...]
     start = 0
     for ref, act in zip(grads, acts):
         stop = start + ref.shape[1]
         act_ref[:, start:stop] = act[...]
         high, low = split(ref[...] * inverse_ref[:, :1])
-        rows = dot(one_hot, high) + dot(one_hot, low)
-        for step, out in enumerate(outs):
-            out[:, start:stop] = rows[step * width : (step + 1) * width]
+        first = ((0,), (0,))
+        rows_ref[:, start:stop] = dot(one_hot, high, first) + dot(one_hot, low, first)
         start = stop
+    for step, out in enumerate(outs):
+        source = lax.rem(grp_ref[0] + (groups - step), groups)
+        out[...] = rows_ref[pl.ds(pl.multiple_of(source * width, width), width), :]
 
 
 def last_kernel(start, stage, grp_ref, *refs):
@@ -254,8 +258,12 @@
     run = 0
     while run < len(stages) and stages[run][1][1] == stages[0][1][1]:
         run += 1
+    flip, shift = divmod(shift, 3)
     shift %= run
-    return stages[shift:run] + stages[:shift] + stages[run:]
+    front = stages[shift:run] + stages[:shift]
+    if flip:
+        front = front[:1] + front[:0:-1]
+    return front + stages[run:]
 
 
 def moved(grp, dev, stage, amount):
@@ -360,18 +368,19 @@
             pltpu.SemaphoreType.DMA((2 + pieces,)),
         ],
     )(in_hbm(feats), in_hbm(local_adj), in_hbm(weight))
-    agg, inverse, hot, *flipped = call(
+    agg_high, agg_low, inverse, hot, *flipped = call(
         functools.partial(aggregate_kernel, groups, share, orders),
-        [
-            shape((nodes, lanes), F32),
-            shape((nodes, LANES), F32),
-            shape((slots, nodes), BF16),
-        ]
+        [shape((nodes, lanes), BF16)] * 2
+        + [shape((nodes, LANES), F32), shape((nodes, slots), BF16)]
         + [shape((inner * share, nodes), F32)] * pair,
-        [SMEM, SMEM, SMEM] + [VMEM] * (2 + groups),
+        [SMEM, SMEM] + [VMEM] * (3 + groups),
         4 * slots * nodes * lanes,
         nodes * lanes * 16,
-        [pltpu.VMEM((lanes, nodes), F32), pltpu.VMEM((slots, nodes), F32)],
+        [
+            pltpu.VMEM((lanes, nodes), F32),
+            pltpu.VMEM((slots, lanes + LANES), F32),
+            pltpu.VMEM((nodes, slots), F32),
+        ],
     )(me, dev, far_row.reshape(groups, width), base, degree, *received)
 
     def to_partner(value, k):
@@ -388,10 +397,10 @@
         act, grad = call(
             functools.partial(forward_kernel, edges[c]),
             [shape((nodes, piece), BF16), shape((nodes, piece), F32)],
-            [VMEM] * 4,
+            [VMEM] * 5,
             6 * nodes * lanes * piece,
             lanes * piece * 4 + nodes * lanes * 4,
-        )(agg, high, low, cotangent)
+        )(agg_high, agg_low, high, low, cotangent)
         acts.append(act)
         grads.append(grad)
     for c in range(CHUNKS):
@@ -439,13 +448,14 @@
         totals.append(keep)
 
     pick_slots = call(
-        functools.partial(slots_kernel, width),
+        functools.partial(slots_kernel, width, groups),
         [shape((width, outer), F32)] * groups + [shape((nodes, outer), BF16)],
-        [VMEM] * (2 + 2 * CHUNKS),
+        [SMEM] + [VMEM] * (2 + 2 * CHUNKS),
         4 * slots * nodes * outer,
         nodes * outer * 4,
+        [pltpu.VMEM((slots, outer), F32)],
     )
-    *slot_rows, activated = pick_slots(hot, inverse, *grads, *acts)
+    *slot_rows, activated = pick_slots(me, hot, inverse, *grads, *acts)
     weight_grad = None
     for c in range(CHUNKS):
         stage = scatter[0][1]

time: 66.9 us -> 66.4 us (level)
  transfers between devices with their start and end apart: 19 -> 19, of which waited for: 8 -> 9; matrix products, arithmetic and copies ran while one was open for 0% -> 0% of each run, Pallas kernels for 19% -> 19%
where the time goes in v3:
time: 66.4 us; the launch traced here: 66.2 us
  waiting for transfers between devices  26.5 us (40%)
  starting transfers between devices  22.5 us (34%)
  Pallas kernels  16 us (24%)
  between operations  0.81 us (1%)
    ppermute x19, waiting for transfers between devices, permute(): return lax.ppermute(value, AXES, pairs)  26.5 us
    ppermute x19, starting transfers between devices, permute(): return lax.ppermute(value, AXES, pairs)  22.5 us
    pallas_call x1, Pallas kernels, body(): back(me, local_adj, mask, inverse, high, low, *grads, *returned)  3.58 us
    pallas_call x1, Pallas kernels, body(): call(functools.partial(local_kernel, pieces), [shape((nodes, lanes), F32)...  2.66 us
    pallas_call x2, Pallas kernels, body(): call(functools.partial(forward_kernel, edges[c]), [shape((nodes, piece),...  2.34 us
    pallas_call x2, Pallas kernels, body(): call(functools.partial(term_kernel, pair, rows, functools.partial(places,...  2.14 us
    pallas_call x2, Pallas kernels, body(): call(functools.partial(last_kernel, edges[c], stage), shape((share, outer...  1.47 us
    pallas_call x1, Pallas kernels, body(): call(functools.partial(border_kernel, groups, width), [shape((width, lane...  1.45 us
  transfers between devices with their start and end apart: 19, of which 9 were waited for; matrix products, arithmetic and copies ran while one was open for 0% of the time, Pallas kernels for 19%

profile of v3, /device:TPU:0, one launch (start us, length us, event | category | flops | bytes accessed | tf_op | source)
XLA Modules:
  0.0 66.2 jit_solution(18408793743564169752)
XLA Ops:
  0.6 1.5 %shard_map.86 = (f32[8,1152]{1,0:T(8,128)S(1)}, f32[8,1152]{1,0:T(8,128)S(1)}, f32[8,1152]{1,0:T(8,128)S(1)}, f32[8,1152]{1,0:T(8,128)S(1)}) custom-call(s32[1]{0:T(128)} %bitcast.me_ref.grp_ref, bf16[256,1024]{1,0:T(8,128)(2,1)} %feats_hbm.3, s32[32,256]{1,0:T(8,128)} %bitcast.4), custom_call_target="tpu_custom_call" | custom-call | flops 16777216 | bytes 557056 | tf_op jit(solution)/shard_map/pallas_call | solution.py:341
  2.1 3.1 %collective-permute-start = (f32[8,1152]{1,0:T(8,128)S(1)}, f32[8,1152]{1,0:T(8,128)S(1)}, u32[]{:S(2)}, u32[]{:S(2)}) collective-permute-start(f32[8,1152]{1,0:T(8,128)S(1)} %get-tuple-element.33), channel_id=1, source_target_pairs={{0,8},{1,9},{2,10},{3,11},{4,12},{5,13},{6,14},{7,15},{8,16},{9,17... | collective-permute-start | bytes 110600 | tf_op jit(solution)/shard_map/ppermute | solution.py:297
  5.2 2.6 %collective-permute-start.1 = (f32[8,1152]{1,0:T(8,128)S(1)}, f32[8,1152]{1,0:T(8,128)S(1)}, u32[]{:S(2)}, u32[]{:S(2)}) collective-permute-start(f32[8,1152]{1,0:T(8,128)S(1)} %get-tuple-element.34), channel_id=1, source_target_pairs={{0,16},{1,17},{2,18},{3,19},{4,20},{5,21},{6,22},{7,23},{8,24},{9,... | collective-permute-start | bytes 110600 | tf_op jit(solution)/shard_map/ppermute | solution.py:297
  7.8 1.3 %collective-permute-start.2 = (f32[8,1152]{1,0:T(8,128)S(1)}, f32[8,1152]{1,0:T(8,128)S(1)}, u32[]{:S(2)}, u32[]{:S(2)}) collective-permute-start(f32[8,1152]{1,0:T(8,128)S(1)} %get-tuple-element.35), channel_id=1, source_target_pairs={{0,24},{1,25},{2,26},{3,27},{4,28},{5,29},{6,30},{7,31},{8,0},{9,1... | collective-permute-start | bytes 110600 | tf_op jit(solution)/shard_map/ppermute | solution.py:297
  9.1 0.0 copy-start.3
  9.1 0.0 copy-start
  9.1 2.7 %shard_map.85 = (f32[256,1024]{1,0:T(8,128)S(1)}, f32[256,128]{1,0:T(8,128)S(1)}, bf16[1024,1024]{1,0:T(8,128)(2,1)S(1)}, bf16[1024,1024]{1,0:T(8,128)(2,1)S(1)}) custom-call(bf16[256,1024]{1,0:T(8,128)(2,1)} %feats_hbm.3, s32[256,256]{1,0:T(8,128)} %adj_ref.1, f32[1024,1024]{1,0:T(8,128)} %weight_hbm.1), custom_call_target="tpu_custom_call" | custom-call | flops 134217728 | bytes 9961472 | tf_op jit(solution)/shard_map/pallas_call | solution.py:357
  11.8 0.0 collective-permute-done.refs_1_
  11.8 0.0 collective-permute-done.1.refs_2_
  11.8 0.0 collective-permute-done.2.refs_3_
  11.8 0.0 copy-done.3
  11.8 1.3 %shard_map.87 = (bf16[256,1024]{1,0:T(8,128)(2,1)S(1)}, bf16[256,1024]{1,0:T(8,128)(2,1)S(1)}, f32[256,128]{1,0:T(8,128)S(1)}, bf16[256,32]{1,0:T(8,128)(2,1)S(1...) custom-call(s32[1]{0:T(128)} %bitcast.me_ref.grp_ref, s32[1]{0:T(128)} %bitcast.1.dev_ref, s32[4,8]{1,0:T(4,128)S(1)} %bitcast.6, ...), custom_call_target="tpu_custom_call" | custom-call | flops 33554432 | bytes 4194304 | tf_op jit(solution)/shard_map/pallas_call | solution.py:371
  13.1 0.1 collective-permute-start.6
  13.2 0.0 copy-done
  13.2 1.2 %shard_map.89 = (bf16[256,512]{1,0:T(8,128)(2,1)S(1)}, f32[256,512]{1,0:T(8,128)S(1)}) custom-call(bf16[256,1024]{1,0:T(8,128)(2,1)S(1)} %get-tuple-element.38.agg_high_ref, bf16[256,1024]{1,0:T(8,128)(2,1)S(1)} %get-tuple-element.39.agg_low_ref, bf16[1024,1024]{1,0:T(8,128)(2,1)S(1)} %get-tuple-element.40.high_ref, ...), custom_call_target="tpu_custom_call" | custom-call | flops 805306368 | bytes 3145728 | tf_op jit(solution)/shard_map/pallas_call | solution.py:397
  14.4 0.6 collective-permute-start.7
  14.9 1.2 %shard_map.88 = (bf16[256,512]{1,0:T(8,128)(2,1)S(1)}, f32[256,512]{1,0:T(8,128)S(1)}) custom-call(bf16[256,1024]{1,0:T(8,128)(2,1)S(1)} %get-tuple-element.38.agg_high_ref, bf16[256,1024]{1,0:T(8,128)(2,1)S(1)} %get-tuple-element.39.agg_low_ref, bf16[1024,1024]{1,0:T(8,128)(2,1)S(1)} %get-tuple-element.40.high_ref, ...), custom_call_target="tpu_custom_call" | custom-call | flops 805306368 | bytes 3145728 | tf_op jit(solution)/shard_map/pallas_call | solution.py:397
  16.1 0.1 collective-permute-start.13
  16.2 0.0 collective-permute-done.6.refs_1_
  16.2 0.3 collective-permute-done.7.refs_3_
  16.5 1.1 %shard_map.92 = (f32[256,512]{1,0:T(8,128)S(1)}, f32[256,512]{1,0:T(8,128)S(1)}) custom-call(s32[1]{0:T(128)} %bitcast.me_ref.grp_ref, s32[1]{0:T(128)} %bitcast.1.dev_ref, f32[512,256]{1,0:T(8,128)S(1)} %get-tuple-element.51.refs_0_, f32[512,256]{1,0:T(8,128)S(1)} %collective-permute-done.6.refs_1_, f32[256,512]{1,0:T(8,128)S(1)} %get-tuple-element.43.refs_1_.refs_2_, ...), custom_call_target="tpu_custom_call" | custom-call | flops 805306368 | bytes 3145728 | tf_op jit(solution)/shard_map/pallas_call | solution.py:409
  17.5 1.6 %collective-permute-start.8 = (f32[256,512]{1,0:T(8,128)S(1)}, f32[256,512]{1,0:T(8,128)S(1)}, u32[]{:S(2)}, u32[]{:S(2)}) collective-permute-start(f32[256,512]{1,0:T(8,128)S(1)} %get-tuple-element.54), channel_id=1, source_target_pairs={{0,2},{1,9},{2,0},{3,11},{4,6},{5,13},{6,4},{7,15},{8,10},{9,1},{1... | collective-permute-start | bytes 1572872 | tf_op jit(solution)/shard_map/ppermute | solution.py:297
  19.1 0.0 collective-permute-done.13.refs_3_
  19.1 1.1 %shard_map.93 = (f32[256,512]{1,0:T(8,128)S(1)}, f32[256,512]{1,0:T(8,128)S(1)}) custom-call(s32[1]{0:T(128)} %bitcast.me_ref.grp_ref, s32[1]{0:T(128)} %bitcast.1.dev_ref, f32[512,256]{1,0:T(8,128)S(1)} %get-tuple-element.51.refs_0_, f32[512,256]{1,0:T(8,128)S(1)} %collective-permute-done.6.refs_1_, f32[256,512]{1,0:T(8,128)S(1)} %get-tuple-element.42.refs_0_.refs_2_, ...), custom_call_target="tpu_custom_call" | custom-call | flops 805306368 | bytes 3145728 | tf_op jit(solution)/shard_map/pallas_call | solution.py:409
  20.2 1.6 %collective-permute-start.14 = (f32[256,512]{1,0:T(8,128)S(1)}, f32[256,512]{1,0:T(8,128)S(1)}, u32[]{:S(2)}, u32[]{:S(2)}) collective-permute-start(f32[256,512]{1,0:T(8,128)S(1)} %get-tuple-element.56), channel_id=1, source_target_pairs={{0,4},{1,3},{2,6},{3,1},{4,0},{5,7},{6,2},{7,5},{8,12},{9,11},{10,... | collective-permute-start | bytes 1572872 | tf_op jit(solution)/shard_map/ppermute | solution.py:297
  21.8 9.7 %collective-permute-done.8 = f32[256,512]{1,0:T(8,128)S(1)} collective-permute-done((f32[256,512]{1,0:T(8,128)S(1)}, f32[256,512]{1,0:T(8,128)S(1)}, u32[]{:S(2)}, u32[]{:S(2)}) %collective-permute-start.8) | collective-permute-done | bytes 524320 | tf_op jit(solution)/shard_map/ppermute | solution.py:297
  31.4 0.1 slice_add_fusion.3
  31.5 0.1 collective-permute-start.9
  31.6 0.0 collective-permute-done.14
  31.6 0.1 slice_add_fusion.1
  31.7 1.6 %collective-permute-start.15 = (f32[128,512]{1,0:T(8,128)S(1)}, f32[128,512]{1,0:T(8,128)S(1)}, u32[]{:S(2)}, u32[]{:S(2)}) collective-permute-start(f32[128,512]{1,0:T(8,128)S(1)} %get-tuple-element.58), channel_id=1, source_target_pairs={{0,2},{1,9},{2,0},{3,11},{4,6},{5,13},{6,4},{7,15},{8,10},{9,1},{1... | collective-permute-start | bytes 786440 | tf_op jit(solution)/shard_map/ppermute | solution.py:297
  33.3 7.3 %collective-permute-done.9 = f32[128,512]{1,0:T(8,128)S(1)} collective-permute-done((f32[128,512]{1,0:T(8,128)S(1)}, f32[128,512]{1,0:T(8,128)S(1)}, u32[]{:S(2)}, u32[]{:S(2)}) %collective-permute-start.9) | collective-permute-done | bytes 262176 | tf_op jit(solution)/shard_map/ppermute | solution.py:297
  40.6 0.0 copy-start.1
  40.6 0.0 copy-start.2
  40.6 1.6 %collective-permute-start.10 = (f32[64,512]{1,0:T(8,128)S(1)}, f32[64,512]{1,0:T(8,128)S(1)}, u32[]{:S(2)}, u32[]{:S(2)}) collective-permute-start(f32[64,512]{1,0:T(8,128)S(1)} %slice_add_fusion.6), channel_id=1, source_target_pairs={{0,4},{1,3},{2,6},{3,1},{4,0},{5,7},{6,2},{7,5},{8,12},{9,11},{10,... | collective-permute-start | bytes 393224 | tf_op jit(solution)/shard_map/ppermute | solution.py:297
  42.2 0.0 collective-permute-done.15
  42.3 0.1 collective-permute-start.16
  42.3 3.7 %collective-permute-done.10 = f32[64,512]{1,0:T(8,128)S(1)} collective-permute-done((f32[64,512]{1,0:T(8,128)S(1)}, f32[64,512]{1,0:T(8,128)S(1)}, u32[]{:S(2)}, u32[]{:S(2)}) %collective-permute-start.10) | collective-permute-done | bytes 131104 | tf_op jit(solution)/shard_map/ppermute | solution.py:297
  46.0 2.0 %collective-permute-start.11 = (f32[64,512]{1,0:T(8,128)S(1)}, f32[64,512]{1,0:T(8,128)S(1)}, u32[]{:S(2)}, u32[]{:S(2)}) collective-permute-start(f32[64,512]{1,0:T(8,128)S(1)} %fusion.1), channel_id=1, source_target_pairs={{0,16},{1,17},{2,18},{3,19},{4,20},{5,21},{6,22},{7,23},{8,24},{9,... | collective-permute-start | bytes 393224 | tf_op jit(solution)/shard_map/ppermute | solution.py:297
  48.1 0.3 collective-permute-done.16
  48.4 1.2 %collective-permute-start.17 = (f32[64,512]{1,0:T(8,128)S(1)}, f32[64,512]{1,0:T(8,128)S(1)}, u32[]{:S(2)}, u32[]{:S(2)}) collective-permute-start(f32[64,512]{1,0:T(8,128)S(1)} %fusion), channel_id=1, source_target_pairs={{0,16},{1,17},{2,18},{3,19},{4,20},{5,21},{6,22},{7,23},{8,24},{9,... | collective-permute-start | bytes 393224 | tf_op jit(solution)/shard_map/ppermute | solution.py:297
  49.6 1.1 %shard_map.90 = (f32[8,1024]{1,0:T(8,128)S(1)}, f32[8,1024]{1,0:T(8,128)S(1)}, f32[8,1024]{1,0:T(8,128)S(1)}, f32[8,1024]{1,0:T(8,128)S(1)}, bf16[256,1024]{1,0:T(8,128)(2,1)}) custom-call(s32[1]{0:T(128)} %bitcast.me_ref.grp_ref, bf16[256,32]{1,0:T(8,128)(2,1)S(1)} %get-tuple-element.36.hot_ref, f32[256,128]{1,0:T(8,128)S(1)} %get-tuple-element.37.inverse_ref, ...), custom_call_target="tpu_custom_call" | custom-call | flops 33554432 | bytes 1048576 | tf_op jit(solution)/shard_map/pallas_call | solution.py:458
  50.8 2.4 %collective-permute-start.3 = (f32[8,1024]{1,0:T(8,128)S(1)}, f32[8,1024]{1,0:T(8,128)S(1)}, u32[]{:S(2)}, u32[]{:S(2)}) collective-permute-start(f32[8,1024]{1,0:T(8,128)S(1)} %get-tuple-element.48), channel_id=1, source_target_pairs={{0,24},{1,25},{2,26},{3,27},{4,28},{5,29},{6,30},{7,31},{8,0},{9,1... | collective-permute-start | bytes 98312 | tf_op jit(solution)/shard_map/ppermute | solution.py:297
  53.1 1.9 %collective-permute-start.4 = (f32[8,1024]{1,0:T(8,128)S(1)}, f32[8,1024]{1,0:T(8,128)S(1)}, u32[]{:S(2)}, u32[]{:S(2)}) collective-permute-start(f32[8,1024]{1,0:T(8,128)S(1)} %get-tuple-element.49), channel_id=1, source_target_pairs={{0,16},{1,17},{2,18},{3,19},{4,20},{5,21},{6,22},{7,23},{8,24},{9,... | collective-permute-start | bytes 98312 | tf_op jit(solution)/shard_map/ppermute | solution.py:297
  55.1 0.0 collective-permute-start.5
  55.1 1.9 %collective-permute-done.11 = f32[64,512]{1,0:T(8,128)S(1)} collective-permute-done((f32[64,512]{1,0:T(8,128)S(1)}, f32[64,512]{1,0:T(8,128)S(1)}, u32[]{:S(2)}, u32[]{:S(2)}) %collective-permute-start.11) | collective-permute-done | bytes 131104 | tf_op jit(solution)/shard_map/ppermute | solution.py:297
  57.0 0.4 collective-permute-start.12
  57.4 1.4 %collective-permute-done.17 = f32[64,512]{1,0:T(8,128)S(1)} collective-permute-done((f32[64,512]{1,0:T(8,128)S(1)}, f32[64,512]{1,0:T(8,128)S(1)}, u32[]{:S(2)}, u32[]{:S(2)}) %collective-permute-start.17) | collective-permute-done | bytes 131104 | tf_op jit(solution)/shard_map/ppermute | solution.py:297
  58.9 0.3 collective-permute-start.18
  59.2 0.0 collective-permute-done.3.refs_3_
  59.2 0.4 collective-permute-done.4.refs_4_
  59.5 1.6 %collective-permute-done.5.refs_5_ = f32[8,1024]{1,0:T(8,128)S(1)} collective-permute-done((f32[8,1024]{1,0:T(8,128)S(1)}, f32[8,1024]{1,0:T(8,128)S(1)}, u32[]{:S(2)}, u32[]{:S(2)}) %collective-permute-start.5) | collective-permute-done | bytes 32800 | tf_op jit(solution)/shard_map/ppermute | solution.py:297
  61.1 0.0 copy-done.1
  61.1 0.0 copy-done.2
  61.1 3.6 %shard_map.91 = f32[256,1024]{1,0:T(8,128)} custom-call(s32[1]{0:T(128)} %bitcast.me_ref.grp_ref, s32[256,256]{1,0:T(8,128)S(1)} %copy-done.1, s32[32,256]{1,0:T(8,128)S(1)} %bitcast.5, f32[256,128]{1,0:T(8,128)S(1)} %get-tuple-element.37.inverse_ref, bf16[1024,1024]{1,0:T(8,128)(2,1)S(1)} %get-tuple-element.40.high_ref, ...), custom_call_target="tpu_custom_call" | custom-call | flops 1610612736 | bytes 6291456 | tf_op jit(solution)/shard_map/pallas_call | solution.py:488
  64.7 0.0 collective-permute-done.18.refs_1_
  64.7 0.7 %shard_map.94.refs_2_ = f32[128,1024]{1,0:T(8,128)} custom-call(s32[1]{0:T(128)} %bitcast.me_ref.grp_ref, f32[64,512]{1,0:T(8,128)S(1)} %add.47.refs_0_, f32[64,512]{1,0:T(8,128)S(1)} %collective-permute-done.18.refs_1_), custom_call_target="tpu_custom_call" | custom-call | flops 65536 | bytes 262144 | tf_op jit(solution)/shard_map/pallas_call | solution.py:468
  65.5 0.0 collective-permute-done.12.refs_1_
  65.5 0.7 %shard_map.95 = f32[128,1024]{1,0:T(8,128)} custom-call(s32[1]{0:T(128)} %bitcast.me_ref.grp_ref, f32[64,512]{1,0:T(8,128)S(1)} %add.41.refs_0_, f32[64,512]{1,0:T(8,128)S(1)} %collective-permute-done.12.refs_1_, f32[128,1024]{1,0:T(8,128)} %shard_map.94.refs_2_), custom_call_target="tpu_custom_call", output_to_operand_aliasing={{}: (3, {})} | custom-call | flops 65536 | bytes 262144 | tf_op jit(solution)/shard_map/pallas_call | solution.py:468
  (6 shorter events, 0.1 us)
Async XLA Ops:
  2.1 9.7 %collective-permute-start = (f32[8,1152]{1,0:T(8,128)S(1)}, f32[8,1152]{1,0:T(8,128)S(1)}, u32[]{:S(2)}, u32[]{:S(2)}) collective-permute-start(f32[8,1152]{1,0:T(8,128)S(1)} %get-tuple-element.33), channel_id=1, source_target_pairs={{0,8},{1,9},{2,10},{3,11},{4,12},{5,13},{6,14},{7,15},{8,16},{9,17... | collective-permute-start | bytes 110600 | tf_op jit(solution)/shard_map/ppermute | solution.py:297
  5.2 6.6 %collective-permute-start.1 = (f32[8,1152]{1,0:T(8,128)S(1)}, f32[8,1152]{1,0:T(8,128)S(1)}, u32[]{:S(2)}, u32[]{:S(2)}) collective-permute-start(f32[8,1152]{1,0:T(8,128)S(1)} %get-tuple-element.34), channel_id=1, source_target_pairs={{0,16},{1,17},{2,18},{3,19},{4,20},{5,21},{6,22},{7,23},{8,24},{9,... | collective-permute-start | bytes 110600 | tf_op jit(solution)/shard_map/ppermute | solution.py:297
  7.8 4.0 %collective-permute-start.2 = (f32[8,1152]{1,0:T(8,128)S(1)}, f32[8,1152]{1,0:T(8,128)S(1)}, u32[]{:S(2)}, u32[]{:S(2)}) collective-permute-start(f32[8,1152]{1,0:T(8,128)S(1)} %get-tuple-element.35), channel_id=1, source_target_pairs={{0,24},{1,25},{2,26},{3,27},{4,28},{5,29},{6,30},{7,31},{8,0},{9,1... | collective-permute-start | bytes 110600 | tf_op jit(solution)/shard_map/ppermute | solution.py:297
  9.1 2.7 %copy-start.3 = (s32[1,1,4,8]{3,2,1,0:T(4,128)S(1)}, s32[1,1,4,8]{3,2,1,0:T(4,128)}, u32[]{:S(2)}) copy-start(s32[1,1,4,8]{3,2,1,0:T(4,128)} %param.11) | copy-start | bytes 388
  9.1 4.0 %copy-start = (bf16[256,1024]{1,0:T(8,128)(2,1)S(1)}, bf16[256,1024]{1,0:T(8,128)(2,1)}, u32[]{:S(2)}) copy-start(bf16[256,1024]{1,0:T(8,128)(2,1)} %cot_ref.3) | copy-start | bytes 1572868
  13.1 3.1 %collective-permute-start.6 = (f32[512,256]{1,0:T(8,128)S(1)}, f32[512,256]{1,0:T(8,128)S(1)}, u32[]{:S(2)}, u32[]{:S(2)}) collective-permute-start(f32[512,256]{1,0:T(8,128)S(1)} %get-tuple-element.52), channel_id=1, source_target_pairs={{0,1},{1,0},{2,3},{3,2},{4,5},{5,4},{6,7},{7,6},{8,9},{9,8},{10,11... | collective-permute-start | bytes 1572872 | tf_op jit(solution)/shard_map/ppermute | solution.py:297
  14.4 2.1 %collective-permute-start.7 = (f32[256,512]{1,0:T(8,128)S(1)}, f32[256,512]{1,0:T(8,128)S(1)}, u32[]{:S(2)}, u32[]{:S(2)}) collective-permute-start(f32[256,512]{1,0:T(8,128)S(1)} %get-tuple-element.43.refs_1_.refs_2_), channel_id=1, source_target_pairs={{0,1},{1,0},{2,3},{3,2},{4,5},{5,4},{6,7},{7,6},{8,9},{9,8},{10,11... | collective-permute-start | bytes 1572872 | tf_op jit(solution)/shard_map/ppermute | solution.py:297
  16.1 3.0 %collective-permute-start.13 = (f32[256,512]{1,0:T(8,128)S(1)}, f32[256,512]{1,0:T(8,128)S(1)}, u32[]{:S(2)}, u32[]{:S(2)}) collective-permute-start(f32[256,512]{1,0:T(8,128)S(1)} %get-tuple-element.42.refs_0_.refs_2_), channel_id=1, source_target_pairs={{0,1},{1,0},{2,3},{3,2},{4,5},{5,4},{6,7},{7,6},{8,9},{9,8},{10,11... | collective-permute-start | bytes 1572872 | tf_op jit(solution)/shard_map/ppermute | solution.py:297
  17.5 13.9 %collective-permute-start.8 = (f32[256,512]{1,0:T(8,128)S(1)}, f32[256,512]{1,0:T(8,128)S(1)}, u32[]{:S(2)}, u32[]{:S(2)}) collective-permute-start(f32[256,512]{1,0:T(8,128)S(1)} %get-tuple-element.54), channel_id=1, source_target_pairs={{0,2},{1,9},{2,0},{3,11},{4,6},{5,13},{6,4},{7,15},{8,10},{9,1},{1... | collective-permute-start | bytes 1572872 | tf_op jit(solution)/shard_map/ppermute | solution.py:297
  20.2 11.5 %collective-permute-start.14 = (f32[256,512]{1,0:T(8,128)S(1)}, f32[256,512]{1,0:T(8,128)S(1)}, u32[]{:S(2)}, u32[]{:S(2)}) collective-permute-start(f32[256,512]{1,0:T(8,128)S(1)} %get-tuple-element.56), channel_id=1, source_target_pairs={{0,4},{1,3},{2,6},{3,1},{4,0},{5,7},{6,2},{7,5},{8,12},{9,11},{10,... | collective-permute-start | bytes 1572872 | tf_op jit(solution)/shard_map/ppermute | solution.py:297
  31.5 9.1 %collective-permute-start.9 = (f32[128,512]{1,0:T(8,128)S(1)}, f32[128,512]{1,0:T(8,128)S(1)}, u32[]{:S(2)}, u32[]{:S(2)}) collective-permute-start(f32[128,512]{1,0:T(8,128)S(1)} %get-tuple-element.60), channel_id=1, source_target_pairs={{0,8},{1,5},{2,10},{3,7},{4,12},{5,1},{6,14},{7,3},{8,0},{9,13},{1... | collective-permute-start | bytes 786440 | tf_op jit(solution)/shard_map/ppermute | solution.py:297
  31.7 10.5 %collective-permute-start.15 = (f32[128,512]{1,0:T(8,128)S(1)}, f32[128,512]{1,0:T(8,128)S(1)}, u32[]{:S(2)}, u32[]{:S(2)}) collective-permute-start(f32[128,512]{1,0:T(8,128)S(1)} %get-tuple-element.58), channel_id=1, source_target_pairs={{0,2},{1,9},{2,0},{3,11},{4,6},{5,13},{6,4},{7,15},{8,10},{9,1},{1... | collective-permute-start | bytes 786440 | tf_op jit(solution)/shard_map/ppermute | solution.py:297
  40.6 20.5 %copy-start.1 = (s32[256,256]{1,0:T(8,128)S(1)}, s32[256,256]{1,0:T(8,128)}, u32[]{:S(2)}) copy-start(s32[256,256]{1,0:T(8,128)} %adj_ref.1) | copy-start | bytes 786436
  40.6 20.5 %copy-start.2 = (s32[1,1,4,8,256]{4,3,2,1,0:T(8,128)S(1)}, s32[1,1,4,8,256]{4,3,2,1,0:T(8,128)}, u32[]{:S(2)}) copy-start(s32[1,1,4,8,256]{4,3,2,1,0:T(8,128)} %param.10) | copy-start | bytes 98308
  40.6 5.4 %collective-permute-start.10 = (f32[64,512]{1,0:T(8,128)S(1)}, f32[64,512]{1,0:T(8,128)S(1)}, u32[]{:S(2)}, u32[]{:S(2)}) collective-permute-start(f32[64,512]{1,0:T(8,128)S(1)} %slice_add_fusion.6), channel_id=1, source_target_pairs={{0,4},{1,3},{2,6},{3,1},{4,0},{5,7},{6,2},{7,5},{8,12},{9,11},{10,... | collective-permute-start | bytes 393224 | tf_op jit(solution)/shard_map/ppermute | solution.py:297
  42.3 6.1 %collective-permute-start.16 = (f32[64,512]{1,0:T(8,128)S(1)}, f32[64,512]{1,0:T(8,128)S(1)}, u32[]{:S(2)}, u32[]{:S(2)}) collective-permute-start(f32[64,512]{1,0:T(8,128)S(1)} %slice_add_fusion.4), channel_id=1, source_target_pairs={{0,8},{1,5},{2,10},{3,7},{4,12},{5,1},{6,14},{7,3},{8,0},{9,13},{1... | collective-permute-start | bytes 393224 | tf_op jit(solution)/shard_map/ppermute | solution.py:297
  46.0 10.9 %collective-permute-start.11 = (f32[64,512]{1,0:T(8,128)S(1)}, f32[64,512]{1,0:T(8,128)S(1)}, u32[]{:S(2)}, u32[]{:S(2)}) collective-permute-start(f32[64,512]{1,0:T(8,128)S(1)} %fusion.1), channel_id=1, source_target_pairs={{0,16},{1,17},{2,18},{3,19},{4,20},{5,21},{6,22},{7,23},{8,24},{9,... | collective-permute-start | bytes 393224 | tf_op jit(solution)/shard_map/ppermute | solution.py:297
  48.4 10.4 %collective-permute-start.17 = (f32[64,512]{1,0:T(8,128)S(1)}, f32[64,512]{1,0:T(8,128)S(1)}, u32[]{:S(2)}, u32[]{:S(2)}) collective-permute-start(f32[64,512]{1,0:T(8,128)S(1)} %fusion), channel_id=1, source_target_pairs={{0,16},{1,17},{2,18},{3,19},{4,20},{5,21},{6,22},{7,23},{8,24},{9,... | collective-permute-start | bytes 393224 | tf_op jit(solution)/shard_map/ppermute | solution.py:297
  50.8 8.4 %collective-permute-start.3 = (f32[8,1024]{1,0:T(8,128)S(1)}, f32[8,1024]{1,0:T(8,128)S(1)}, u32[]{:S(2)}, u32[]{:S(2)}) collective-permute-start(f32[8,1024]{1,0:T(8,128)S(1)} %get-tuple-element.48), channel_id=1, source_target_pairs={{0,24},{1,25},{2,26},{3,27},{4,28},{5,29},{6,30},{7,31},{8,0},{9,1... | collective-permute-start | bytes 98312 | tf_op jit(solution)/shard_map/ppermute | solution.py:297
  53.1 6.4 %collective-permute-start.4 = (f32[8,1024]{1,0:T(8,128)S(1)}, f32[8,1024]{1,0:T(8,128)S(1)}, u32[]{:S(2)}, u32[]{:S(2)}) collective-permute-start(f32[8,1024]{1,0:T(8,128)S(1)} %get-tuple-element.49), channel_id=1, source_target_pairs={{0,16},{1,17},{2,18},{3,19},{4,20},{5,21},{6,22},{7,23},{8,24},{9,... | collective-permute-start | bytes 98312 | tf_op jit(solution)/shard_map/ppermute | solution.py:297
  55.1 6.1 %collective-permute-start.5 = (f32[8,1024]{1,0:T(8,128)S(1)}, f32[8,1024]{1,0:T(8,128)S(1)}, u32[]{:S(2)}, u32[]{:S(2)}) collective-permute-start(f32[8,1024]{1,0:T(8,128)S(1)} %get-tuple-element.50), channel_id=1, source_target_pairs={{0,8},{1,9},{2,10},{3,11},{4,12},{5,13},{6,14},{7,15},{8,16},{9,17... | collective-permute-start | bytes 98312 | tf_op jit(solution)/shard_map/ppermute | solution.py:297
  57.0 8.5 %collective-permute-start.12 = (f32[64,512]{1,0:T(8,128)S(1)}, f32[64,512]{1,0:T(8,128)S(1)}, u32[]{:S(2)}, u32[]{:S(2)}) collective-permute-start(f32[64,512]{1,0:T(8,128)S(1)} %add.41.refs_0_), channel_id=1, source_target_pairs={{0,8},{1,9},{2,10},{3,11},{4,12},{5,13},{6,14},{7,15},{8,0},{9,1},... | collective-permute-start | bytes 393224 | tf_op jit(solution)/shard_map/ppermute | solution.py:297
  58.9 5.9 %collective-permute-start.18 = (f32[64,512]{1,0:T(8,128)S(1)}, f32[64,512]{1,0:T(8,128)S(1)}, u32[]{:S(2)}, u32[]{:S(2)}) collective-permute-start(f32[64,512]{1,0:T(8,128)S(1)} %add.47.refs_0_), channel_id=1, source_target_pairs={{0,8},{1,9},{2,10},{3,11},{4,12},{5,13},{6,14},{7,15},{8,0},{9,1},... | collective-permute-start | bytes 393224 | tf_op jit(solution)/shard_map/ppermute | solution.py:297
